TPU v7x, 32 devices: a whole 2x2x4 slice. The times are simulated.
32 devices in a mesh: gx: 4 (over z), gy: 8 (over y, x, core).
Axes of the slice: x: 2, y: 2, z: 4, core: 2. Of those that a mesh axis runs over, the one named last changes fastest.
Arguments:
- media: bfloat16 [16384, 1536], P(('gx', 'gy')), may hold values from -6 to 6
- latents: bfloat16 [2048, 1536], P(('gx', 'gy')), may hold values from -6 to 6
- frame_counts: int32 [8, 4], replicated, may hold values from 1 to 8, 16 in all within a row
- time_index: int32 [128], P(('gx', 'gy')), may hold values from 0 to 7
- valid: int32 [16384], P(('gx', 'gy')), may hold values from 0 to 1
- time_table: bfloat16 [8, 1536], P(None, ('gx', 'gy')), may hold values from -3 to 3
- media_gain: bfloat16 [1536], P(('gx', 'gy')), may hold values from 0.5 to 1.5
- latent_gain: bfloat16 [1536], P(('gx', 'gy')), may hold values from 0.5 to 1.5
- ffn_gain: bfloat16 [1536], P(('gx', 'gy')), may hold values from 0.5 to 1.5
- w_query: bfloat16 [1536, 1536], P(('gx', 'gy')), may hold values from -0.3125 to 0.3125
- w_key: bfloat16 [1536, 1536], P(('gx', 'gy')), may hold values from -0.15625 to 0.15625
- w_value: bfloat16 [1536, 1536], P(('gx', 'gy')), may hold values from -0.15625 to 0.15625
- w_out: bfloat16 [1536, 1536], P(('gx', 'gy')), may hold values from -0.625 to 0.625
- w_up: bfloat16 [1536, 6144], P(('gx', 'gy')), may hold values from -0.15625 to 0.15625
- w_down: bfloat16 [6144, 1536], P(('gx', 'gy')), may hold values from -0.078125 to 0.078125
- cotangent: bfloat16 [2048, 1536], P(('gx', 'gy')), may hold values from -6 to 6
Outputs:
- new_latents: bfloat16 [2048, 1536], P(('gx', 'gy'))
- media_grad: float32 [16384, 1536], P(('gx', 'gy'))
- latents_grad: float32 [2048, 1536], P(('gx', 'gy'))
- time_table_grad: float32 [8, 1536], P(None, ('gx', 'gy'))
- media_gain_grad: float32 [1536], P(('gx', 'gy'))
- latent_gain_grad: float32 [1536], P(('gx', 'gy'))
- feedforward_gain_gradient: float32 [1536], P(('gx', 'gy'))
- w_query_grad: float32 [1536, 1536], P(('gx', 'gy'))
- w_key_grad: float32 [1536, 1536], P(('gx', 'gy'))
- w_value_grad: float32 [1536, 1536], P(('gx', 'gy'))
- w_out_grad: float32 [1536, 1536], P(('gx', 'gy'))
- w_up_grad: float32 [1536, 6144], P(('gx', 'gy'))
- w_down_grad: float32 [6144, 1536], P(('gx', 'gy'))
Inputs may be any that keep to these rules, and one draw needn't show every extreme that they name: `frame_counts`: entry (g, j) counts the frames of item j times the number of rows plus g, which lie in order of j; each row sums to 4 times its number of entries and holds one entry of exactly 8.
All inputs are finite; a program needn't handle non-finite values.
Results may differ from a plain program's by a relative error of at most 0.015.
Values may be sent and summed in bfloat16 or wider, within the bound.
A program may use at most 448 MiB of HBM per device.

v0:
```python
from functools import partial

import jax
import jax.numpy as jnp
from jax import lax
from jax.experimental import pallas as pl
from jax.experimental.pallas import tpu as pltpu
from jax.sharding import PartitionSpec as P

H = 16


ENTROPY_WEIGHT = 4.0
NORM_STABILIZER = 1e-05
AXES = ("gx", "gy")
LINES = 4
PLANE = 4
HBM = pl.ANY
BF16 = jnp.bfloat16
F32 = jnp.float32


def here():
    z = lax.axis_index("gx")
    g = lax.axis_index("gy")
    return z, g, g // 2, g % 2


def sibling(g):
    return g + 1 - 2 * (g % 2)


def along_x(g):
    return g + 2 - 4 * ((g // 2) % 2)


def along_y(g):
    return (g + 4) % 8


def turn(z, k):
    return (z + k) % LINES


def greet(devices):
    barrier = pltpu.get_barrier_semaphore()
    for device in devices:
        pl.semaphore_signal(
            barrier, inc=1, device_id=device, device_id_type=pl.DeviceIdType.MESH
        )
    pl.semaphore_wait(barrier, len(devices))


def line_of(z, g):
    return [(turn(z, k), g) for k in (1, 2, 3)]


class Wires:
    def __init__(self, send_sems, recv_sems):
        self.send_sems, self.recv_sems, self.used, self.sent = send_sems, recv_sems, 0, []

    def reserve(self, count):
        first = self.used
        self.used += count
        return first

    def copy(self, source, target, device, send, recv):
        return pltpu.make_async_remote_copy(
            src_ref=source,
            dst_ref=target,
            send_sem=self.send_sems.at[send],
            recv_sem=self.recv_sems.at[recv],
            device_id=device,
            device_id_type=pl.DeviceIdType.MESH,
        )

    def send(self, source, target, device):
        n = self.reserve(1)
        copy = self.copy(source, target, device, n, n)
        copy.start()
        self.sent.append((None, copy))
        return copy

    def send_if(self, condition, source, target, device, send, recv):
        copy = self.copy(source, target, device, send, recv)
        self.sent.append((condition, copy))

        @pl.when(condition)
        def _():
            copy.start()

        return copy

    def drain(self):
        for condition, copy in self.sent:
            if condition is None:
                copy.wait_send()
            else:
                pl.when(condition)(copy.wait_send)


class Line:
    def __init__(self, wires, shard, slot):
        self.wires, self.shard, self.slot = wires, shard, slot
        self.z, self.g, _, _ = here()
        self.base = wires.reserve(4)
        low, high = (3 - self.z) // 3, self.z // 3
        self.order = (1 + 2 * low, 3 - low - high, 2 - low + high)

    def first(self):
        z, g = self.z, self.g
        own = self.slot(z)
        base = self.base
        self.wires.send_if(z < 3, self.shard, own, (turn(z, 1), g), base + 1, base + 1)
        self.wires.send_if(z > 0, self.shard, own, (turn(z, 3), g), base + 3, base + 3)
        self.across = self.wires.copy(self.shard, own, (turn(z, 2), g), base + 2, base + 2)
        self.across.start()
        self.wires.sent.append((None, self.across))

    def take(self, step):
        z, g = self.z, self.g
        k = self.order[step]
        origin = turn(z, LINES - k)
        held = self.slot(origin)
        self.wires.copy(held, held, (z, g), 0, self.base + k).wait_recv()
        if step == 2:
            self.relay(z == 2, 3, 3)
        if step == 2:
            self.relay(z == 1, 0, 1)
        return origin

    def relay(self, condition, there, k):
        held = self.slot(turn(self.z, 2))
        self.wires.send_if(
            condition, held, held, (there, self.g), self.base, self.base + k
        )


class LineSplit:
    def __init__(self, wires, shard, slot):
        self.wires, self.shard, self.slot = wires, shard, slot
        self.z, self.g, _, _ = here()
        self.base = wires.reserve(LINES)
        low, high = (3 - self.z) // 3, self.z // 3
        self.order = (1 + 2 * low, 3 - low - high, 2 - low + high)

    def first(self):
        for k in (2, 1, 3):
            there = turn(self.z, k)
            copy = self.wires.copy(
                piece_of(self.shard, there),
                self.slot(self.z),
                (there, self.g),
                self.base + k,
                self.base + k,
            )
            copy.start()
            self.wires.sent.append((None, copy))

    def take(self, step):
        k = self.order[step]
        origin = turn(self.z, LINES - k)
        held = self.slot(origin)
        self.wires.copy(held, held, (self.z, self.g), 0, self.base + k).wait_recv()
        return origin


def piece_of(shard, place):
    width = shard.shape[-1] // LINES
    return shard.at[:, pl.ds(pl.multiple_of(place * width, 128), width)]


class Spread:
    def __init__(self, wires, shard, slot, half, whole, split=False):
        self.wires, self.shard, self.slot, self.half, self.whole = wires, shard, slot, half, whole
        self.z, self.g, _, _ = here()
        self.line = (LineSplit if split else Line)(wires, shard, lambda z: slot(z, self.g))
        if split:
            self.shard = piece_of(shard, self.z)
        self.zs, self.x, self.y, self.dx, self.dy, self.sib = [self.z], [], [], {}, {}, []

    def side(self, gy):
        return (self.z, gy)

    def to_sibling(self, held):
        if self.whole:
            self.sib.append(self.wires.send(held, held, self.side(sibling(self.g))))

    def first(self):
        own = self.slot(self.z, self.g)
        self.line.first()
        self.x.append(self.wires.send(self.shard, own, self.side(along_x(self.g))))
        self.y.append(self.wires.send(self.shard, own, self.side(along_y(self.g))))
        if self.whole:
            self.sib.append(self.wires.send(self.shard, own, self.side(sibling(self.g))))

    def column(self, step):
        self.zs.append(self.line.take(step))
        held = self.slot(self.zs[-1], self.g)
        self.x.append(self.wires.send(held, held, self.side(along_x(self.g))))
        self.y.append(self.wires.send(held, held, self.side(along_y(self.g))))
        self.to_sibling(held)

    def corner(self, n):
        self.corner_x(n)
        self.corner_y(n)

    def corner_x(self, n):
        self.x[n].wait_recv()
        held = self.slot(self.zs[n], along_x(self.g))
        part = self.half(held, 0)
        self.dy[n] = self.wires.send(part, part, self.side(along_y(self.g)))
        self.to_sibling(held)

    def corner_y(self, n):
        self.y[n].wait_recv()
        held = self.slot(self.zs[n], along_y(self.g))
        part = self.half(held, 1)
        self.dx[n] = self.wires.send(part, part, self.side(along_x(self.g)))
        self.to_sibling(held)

    def last(self, n):
        self.dy[n].wait_recv()
        self.dx[n].wait_recv()
        self.to_sibling(self.slot(self.zs[n], along_y(along_x(self.g))))

    def finish(self):
        for copy in self.sib:
            copy.wait_recv()


def spread_all(flows):
    for flow in flows:
        flow.first()
    for flow in flows:
        flow.corner(0)
    for step in range(3):
        for flow in flows:
            flow.column(step)
        for flow in flows:
            flow.corner(step + 1)
    for n in range(4):
        for flow in flows:
            flow.last(n)
    for flow in flows:
        flow.finish()


LINE_SEMS = 4


def spread_sems(whole):
    return LINE_SEMS + 8 + 8 + (16 if whole else 0)


def columns_half(ref, which):
    width = ref.shape[-1] // 2
    return ref.at[..., pl.ds(which * width, width)]


def rows_half(ref, which):
    rows = ref.shape[0] // 2
    return ref.at[pl.ds(which * rows, rows)]


def rows_parts(ref, which):
    return ref.at[pl.ds(32, 16)] if which else ref.at[pl.ds(0, 32)]


def sides_of(z, g, whole):
    near = [(z, along_x(g)), (z, along_y(g))]
    return near + [(z, sibling(g))] if whole else near


def params(ident):
    return pltpu.CompilerParams(
        collective_id=ident, has_side_effects=True, vmem_limit_bytes=60 * 2**20
    )


def sems(count):
    return pltpu.SemaphoreType.DMA((count,))


VMEM = pl.BlockSpec(memory_space=pltpu.VMEM)
LEFT = pl.BlockSpec(memory_space=HBM)


class SumLine:
    def __init__(self, wires, source, out, relayed=None):
        self.wires, self.source, self.out, self.relayed = wires, source, out, relayed
        self.z, self.g, _, _ = here()
        self.base = wires.reserve(LINES)
        low, high = (3 - self.z) // 3, self.z // 3
        self.back = (0, 1 + 2 * low, 3 - low - high, 2 - low + high)
        self.places = [turn(self.z, LINES - k) if n else self.z for n, k in enumerate(self.back)]
        self.end = low + high > 0
        self.inner = low + high < 1
        self.beside = 1 + high

    def step(self, n):
        place = self.places[n]
        if n < 3 or self.relayed is None:
            k = LINES - self.back[n]
            copy = self.wires.copy(
                self.source.at[place],
                self.out.at[self.z],
                (place, self.g),
                self.base + k,
                self.base + k,
            )
            copy.start()
            self.wires.sent.append((None, copy))
        else:
            self.wires.send_if(
                self.end,
                self.source.at[place],
                self.relayed,
                (self.beside, self.g),
                self.base,
                self.base,
            )

    def first(self):
        for n in (2, 1, 3):
            self.step(n)
        self.clear()
        self.out[self.z] = self.source[self.z]

    def clear(self):
        if self.relayed is None:
            return

        @pl.when(self.end)
        def _():
            self.out[3 - self.z] = jnp.zeros(self.out.shape[1:], self.out.dtype)

    def relay(self):
        place = self.places[3]
        held = self.source.at[place]
        across = self.wires.copy(
            held, self.out.at[self.z], (place, self.g), self.base + 2, self.base + 2
        )
        came = self.wires.copy(
            self.relayed, self.relayed, (self.z, self.g), self.base, self.base
        )
        self.wires.sent.append((self.inner, across))

        @pl.when(self.inner)
        def _():
            came.wait_recv()
            held[...] = held[...] + self.relayed[...]
            across.start()

    def finish(self):
        for k, condition in ((1, self.z > 0), (3, self.z < 3), (2, None)):
            if self.relayed is None:
                condition = None
            held = self.out.at[turn(self.z, LINES - k)]
            copy = self.wires.copy(held, held, (self.z, self.g), 0, self.base + k)
            if condition is None:
                copy.wait_recv()
            else:
                pl.when(condition)(copy.wait_recv)


class Exchange:
    def __init__(self, wires, arrays):
        self.lines = [SumLine(wires, *array) for array in arrays]

    def first(self):
        for line in self.lines:
            line.first()

    def relay(self):
        for line in self.lines:
            line.relay()

    def finish(self):
        for line in self.lines:
            line.finish()


def add_slots(target, source, count):
    @pl.loop(0, count)
    def _(n):
        target[n] = (target[n].astype(F32) + source[n].astype(F32)).astype(target.dtype)


def sum_slots(ref):
    found = ref[0].astype(F32)
    for n in range(1, LINES):
        found = found + ref[n].astype(F32)
    return found


class Fold:
    summed = True

    def __init__(self, wires, parts, whole, scratch, out):
        self.wires, self.parts, self.whole, self.out = wires, parts, whole, out
        self.from_sib, self.cx, self.cy, self.fx, self.fy, self.fz, self.relayed = scratch
        self.z, self.g, self.chip, self.core = here()
        self.cut = self.cy.shape[-1]
        self.lines = SumLine(wires, self.fx, self.fz, self.relayed) if self.summed else None

    def send(self, source, target, gy):
        return self.wires.send(source, target, (self.z, gy))

    def column(self, q):
        return self.parts.at[:, q, self.core] if self.whole else self.parts.at[:, q]

    def half(self, ref, which):
        if which:
            return ref.at[:, :, pl.ds(self.cut, ref.shape[-1] - self.cut)]
        return ref.at[:, :, pl.ds(0, self.cut)]

    def merge(self, q):
        if self.whole:
            core = self.core

            @pl.loop(0, LINES)
            def _(n):
                self.parts[n, q, core] = self.parts[n, q, core] + self.from_sib[n, q]

    def start(self):
        if self.whole:
            theirs = self.parts.at[:, :, 1 - self.core]
            self.sib = self.send(theirs, self.from_sib, sibling(self.g))

    def corner(self):
        if self.whole:
            self.sib.wait_recv()
        q = along_y(along_x(self.g)) // 2
        self.merge(q)
        far = self.column(q)
        self.to_y = self.send(self.half(far, 0), self.cy, along_y(self.g))
        self.to_x = self.send(self.half(far, 1), self.cx, along_x(self.g))

    def side(self, gy, came, corner, which, target):
        q = gy // 2
        self.merge(q)
        came.wait_recv()
        column = self.column(q)
        cols = slice(self.cut, None) if which else slice(0, self.cut)

        @pl.loop(0, LINES)
        def _(n):
            column[n, :, cols] = column[n, :, cols] + corner[n]

        return self.send(column, target, gy)

    def side_x(self):
        self.by_x = self.side(along_x(self.g), self.to_y, self.cy, 0, self.fx)

    def side_y(self):
        self.by_y = self.side(along_y(self.g), self.to_x, self.cx, 1, self.fy)

    def line(self):
        self.merge(self.chip)
        self.by_x.wait_recv()
        self.by_y.wait_recv()
        column = self.column(self.chip)
        for n in (3, 2, 1):
            there = self.lines.places[n]
            self.fx[there] = (
                column[there].astype(F32)
                + self.fx[there].astype(F32)
                + self.fy[there].astype(F32)
            ).astype(BF16)
            self.lines.step(n)
        z = self.z
        self.lines.clear()
        self.fz[z] = jnp.zeros(self.fz.shape[1:], BF16)
        self.out[...] = column[z].astype(F32) + self.fx[z].astype(F32) + self.fy[z].astype(F32)

    def relay(self):
        self.lines.relay()

    def finish(self):
        self.lines.finish()
        self.out[...] += sum_slots(self.fz)


class FoldSplit(Fold):
    summed = False

    def line(self):
        self.merge(self.chip)
        self.by_x.wait_recv()
        self.by_y.wait_recv()
        column = self.column(self.chip)
        self.zs = []
        for k in (2, 1, 3, 0):
            there = turn(self.z, k) if k else self.z
            found = (
                column[there].astype(F32)
                + self.fx[there].astype(F32)
                + self.fy[there].astype(F32)
            ).astype(BF16)
            if k:
                self.fx[there] = found
                self.zs.append(
                    self.wires.send(self.fx.at[there], self.fz.at[self.z], (there, self.g))
                )
            else:
                self.fz[self.z] = found

    def finish(self):
        for copy in self.zs:
            copy.wait_recv()
        width = self.fz.shape[-1]
        for place in range(LINES):
            self.out[:, place * width : (place + 1) * width] = self.fz[place].astype(F32)


def fold_scratch(rows, cols, whole, split=False):
    cut = 256 if split else cols // 2
    return [
        pltpu.VMEM((LINES, PLANE, rows, cols) if whole else (1, 1, 16, 128), BF16),
        pltpu.VMEM((LINES, rows, cols - cut), BF16),
        pltpu.VMEM((LINES, rows, cut), BF16),
        pltpu.VMEM((LINES, rows, cols), BF16),
        pltpu.VMEM((LINES, rows, cols), BF16),
        pltpu.VMEM((LINES, rows, cols), BF16),
        pltpu.VMEM((rows, cols), BF16),
    ]


FOLD = 7


def fold_sems(whole):
    return (1 if whole else 0) + 4 + LINES


class FoldSteps:
    def __init__(self, wires, parts, scratch, out):
        self.wires, self.parts, self.out = wires, parts, out
        _, self.cx, self.cy, self.fx, self.fy, self.fz, relayed = scratch
        self.z, self.g, self.chip, _ = here()
        self.width = parts.shape[-1] // 2
        self.lines = SumLine(wires, self.fx, self.fz, relayed)
        self.zs = self.lines.places
        self.to_x, self.to_y, self.by_x, self.by_y = {}, {}, {}, {}

    def half(self, n, q, which):
        return self.parts.at[self.zs[n], q, :, pl.ds(which * self.width, self.width)]

    def corner(self, n):
        far = along_y(along_x(self.g)) // 2
        place = self.zs[n]
        self.to_y[n] = self.wires.send(
            self.half(n, far, 0), self.cy.at[place], (self.z, along_y(self.g))
        )
        self.to_x[n] = self.wires.send(
            self.half(n, far, 1), self.cx.at[place], (self.z, along_x(self.g))
        )

    def side(self, n, gy, came, corner, which, target):
        came.wait_recv()
        q, place = gy // 2, self.zs[n]
        cols = slice(which * self.width, (which + 1) * self.width)
        self.parts[place, q, :, cols] = self.parts[place, q, :, cols] + corner[place]
        return self.wires.send(self.parts.at[place, q], target.at[place], (self.z, gy))

    def side_x(self, n):
        self.by_x[n] = self.side(n, along_x(self.g), self.to_y[n], self.cy, 0, self.fx)

    def side_y(self, n):
        self.by_y[n] = self.side(n, along_y(self.g), self.to_x[n], self.cx, 1, self.fy)

    def line(self, n):
        self.by_x[n].wait_recv()
        self.by_y[n].wait_recv()
        place = self.zs[n]
        found = (
            self.parts[place, self.chip].astype(F32)
            + self.fx[place].astype(F32)
            + self.fy[place].astype(F32)
        )
        if n == 0:
            self.out[...] = found
            self.lines.clear()
            self.fz[self.z] = jnp.zeros(self.fz.shape[1:], BF16)
        else:
            self.fx[place] = found.astype(BF16)
            self.lines.step(n)

    def relay(self):
        self.lines.relay()

    def finish(self):
        self.lines.finish()
        self.out[...] += sum_slots(self.fz)


STEP_SEMS = 16 + LINES


def layer_norm(row_block, gain_row):
    row_mean = jnp.mean(row_block, axis=-1, keepdims=True)
    centred = row_block - row_mean
    variance = jnp.mean(centred * centred, axis=-1, keepdims=True)
    return centred * lax.rsqrt(variance + NORM_STABILIZER) * gain_row


def product(left_side, right_side):
    return jnp.dot(left_side, right_side, preferred_element_type=jnp.float32)


def inner_first(left_side, right_side):
    return lax.dot_general(
        left_side, right_side, (((0,), (0,)), ((), ())), preferred_element_type=jnp.float32
    )


def inner_last(left_side, right_side):
    return lax.dot_general(
        left_side, right_side, (((1,), (1,)), ((), ())), preferred_element_type=jnp.float32
    )


def collect(onehot_rows, value_rows):
    return lax.dot_general(
        onehot_rows,
        value_rows,
        (((0,), (0,)), ((), ())),
        precision=lax.Precision.HIGHEST,
        preferred_element_type=jnp.float32,
    )


def plain_device(
    media,
    latents,
    frame_counts,
    time_index,
    valid,
    time_table,
    media_gain,
    latent_gain,
    ffn_gain,
    w_query,
    w_key,
    w_value,
    w_out,
    w_up,
    w_down,
    cotangent,
):
    frames = time_index.shape[0]
    patches = valid.shape[0] // frames
    latent_rows = latents.shape[0]
    model_width = latents.shape[1]
    head_size = model_width // H
    score_scale = head_size ** (-0.5)
    across = lax.axis_size("gx")
    column = lax.axis_index("gx")
    row_index = lax.axis_index("gy")
    frame_ends = jnp.cumsum(frame_counts[row_index])
    position = column * frames + jnp.arange(frames, dtype=jnp.int32)
    item_index = jnp.sum((frame_ends[None, :] <= position[:, None]).astype(jnp.int32), axis=1)
    item_onehot = (item_index[:, None] == jnp.arange(across, dtype=jnp.int32)[None, :]).astype(
        jnp.float32
    )
    (
        full_query,
        full_key,
        full_value,
        full_out,
        full_up,
        full_down,
        full_media_gain,
        full_latent_gain,
        full_ffn_gain,
        full_time,
    ) = (
        lax.all_gather(w_query, ("gx", "gy"), axis=0, tiled=True),
        lax.all_gather(w_key, ("gx", "gy"), axis=0, tiled=True),
        lax.all_gather(w_value, ("gx", "gy"), axis=0, tiled=True),
        lax.all_gather(w_out, ("gx", "gy"), axis=0, tiled=True),
        lax.all_gather(w_up, ("gx", "gy"), axis=0, tiled=True),
        lax.all_gather(w_down, ("gx", "gy"), axis=0, tiled=True),
        lax.all_gather(media_gain, ("gx", "gy"), axis=0, tiled=True),
        lax.all_gather(latent_gain, ("gx", "gy"), axis=0, tiled=True),
        lax.all_gather(ffn_gain, ("gx", "gy"), axis=0, tiled=True),
        lax.all_gather(time_table, ("gx", "gy"), axis=1, tiled=True),
    )
    time_onehot = (
        time_index[:, None] == jnp.arange(full_time.shape[0], dtype=jnp.int32)[None, :]
    ).astype(jnp.float32)
    time_rows = product(time_onehot.astype(jnp.bfloat16), full_time)
    media_in = (
        media.astype(jnp.float32).reshape(frames, patches, model_width) + time_rows[:, None, :]
    ).reshape(-1, model_width)
    media_normed = layer_norm(media_in, full_media_gain.astype(jnp.float32)).astype(jnp.bfloat16)
    key_heads = (
        product(media_normed, full_key).astype(jnp.bfloat16).reshape(frames, patches, H, head_size)
    )
    value_heads = (
        product(media_normed, full_value)
        .astype(jnp.bfloat16)
        .reshape(frames, patches, H, head_size)
    )
    latent_in = latents.astype(jnp.float32)
    latent_normed = layer_norm(latent_in, full_latent_gain.astype(jnp.float32)).astype(jnp.bfloat16)
    own_query = product(latent_normed, full_query).astype(jnp.bfloat16)
    own_key = product(latent_normed, full_key).astype(jnp.bfloat16)
    own_value = product(latent_normed, full_value).astype(jnp.bfloat16)
    valid_total = lax.psum(jnp.sum(valid.astype(jnp.float32)), ("gx", "gy"))
    coefficient = ENTROPY_WEIGHT * (valid.shape[0] * lax.axis_size(("gx", "gy"))) / valid_total
    query_table = lax.all_gather(own_query, "gx", axis=0, tiled=True)
    picked = query_table.reshape(-1, latent_rows, H, head_size)[item_index]
    media_score = (
        jnp.einsum("flhd,fphd->flhp", picked, key_heads, preferred_element_type=jnp.float32)
        * score_scale
    )
    valid_mask = valid.reshape(frames, 1, 1, patches) > 0
    media_expo = jnp.where(valid_mask, jnp.exp(media_score), 0.0)
    expo_low = media_expo.astype(jnp.bfloat16)
    media_total = jnp.sum(media_expo, axis=-1)
    media_moment = jnp.sum(media_expo * media_score, axis=-1)
    media_weighted = jnp.einsum(
        "flhp,fphd->flhd", expo_low, value_heads, preferred_element_type=jnp.float32
    )
    dense_weighted = collect(item_onehot, media_weighted.reshape(frames, -1)).reshape(
        -1, model_width
    )
    dense_total = collect(item_onehot, media_total.reshape(frames, -1)).reshape(-1, H)
    dense_moment = collect(item_onehot, media_moment.reshape(frames, -1)).reshape(-1, H)
    got_weighted, got_total, got_moment = (
        lax.psum_scatter(dense_weighted, "gx", scatter_dimension=0, tiled=True),
        lax.psum_scatter(dense_total, "gx", scatter_dimension=0, tiled=True),
        lax.psum_scatter(dense_moment, "gx", scatter_dimension=0, tiled=True),
    )
    query_head_count = own_query.reshape(latent_rows, H, head_size)
    latent_key_rows = own_key.reshape(latent_rows, H, head_size)
    latent_value_rows = own_value.reshape(latent_rows, H, head_size)
    latent_score = (
        jnp.einsum(
            "uer,zer->uez", query_head_count, latent_key_rows, preferred_element_type=jnp.float32
        )
        * score_scale
    )
    latent_expo = jnp.exp(latent_score)
    latent_reduced_precision = latent_expo.astype(jnp.bfloat16)
    weighted = got_weighted.reshape(latent_rows, H, head_size) + jnp.einsum(
        "nwr,rwb->nwb",
        latent_reduced_precision,
        latent_value_rows,
        preferred_element_type=jnp.float32,
    )
    totals = got_total + jnp.sum(latent_expo, axis=-1)
    moment = got_moment + jnp.sum(latent_expo * latent_score, axis=-1)
    attention = weighted / totals[..., None]
    attn_low = attention.reshape(latent_rows, model_width).astype(jnp.bfloat16)
    middle = latent_in + product(attn_low, full_out)
    ffn_normed = layer_norm(middle, full_ffn_gain.astype(jnp.float32)).astype(jnp.bfloat16)
    up_rows = product(ffn_normed, full_up)
    hidden = jax.nn.gelu(up_rows, approximate=False).astype(jnp.bfloat16)
    new_latents = (middle + product(hidden, full_down)).astype(jnp.bfloat16)
    (
        back_query,
        back_key,
        back_value,
        back_out,
        back_up,
        back_down,
        back_media_gain,
        back_latent_gain,
        back_ffn_gain,
    ) = (
        lax.all_gather(w_query, ("gx", "gy"), axis=0, tiled=True),
        lax.all_gather(w_key, ("gx", "gy"), axis=0, tiled=True),
        lax.all_gather(w_value, ("gx", "gy"), axis=0, tiled=True),
        lax.all_gather(w_out, ("gx", "gy"), axis=0, tiled=True),
        lax.all_gather(w_up, ("gx", "gy"), axis=0, tiled=True),
        lax.all_gather(w_down, ("gx", "gy"), axis=0, tiled=True),
        lax.all_gather(media_gain, ("gx", "gy"), axis=0, tiled=True),
        lax.all_gather(latent_gain, ("gx", "gy"), axis=0, tiled=True),
        lax.all_gather(ffn_gain, ("gx", "gy"), axis=0, tiled=True),
    )
    owned_latent, owned_attn, owned_ffn, owned_hidden = (
        lax.all_to_all(latent_normed, ("gx", "gy"), split_axis=1, concat_axis=0, tiled=True),
        lax.all_to_all(attn_low, ("gx", "gy"), split_axis=1, concat_axis=0, tiled=True),
        lax.all_to_all(ffn_normed, ("gx", "gy"), split_axis=1, concat_axis=0, tiled=True),
        lax.all_to_all(hidden, ("gx", "gy"), split_axis=1, concat_axis=0, tiled=True),
    )
    hidden_grad = inner_last(cotangent, back_down)
    gelu_pull = jax.vjp(partial(jax.nn.gelu, approximate=False), up_rows)[1]
    up_grad = gelu_pull(hidden_grad)[0].astype(jnp.bfloat16)
    ffn_normed_grad = inner_last(up_grad, back_up)
    ffn_pull = jax.vjp(layer_norm, middle, back_ffn_gain.astype(jnp.float32))[1]
    middle_part, grad_ffn_gain = ffn_pull(ffn_normed_grad)
    middle_grad = cotangent.astype(jnp.float32) + middle_part
    middle_low = middle_grad.astype(jnp.bfloat16)
    attn_grad = inner_last(middle_low, back_out).reshape(latent_rows, H, head_size)
    weighted_sum_gradient = (attn_grad / totals[..., None]).astype(jnp.bfloat16)
    slope_term = -coefficient / totals
    shift_term = (
        -jnp.sum(attn_grad * attention, axis=-1) / totals
        + coefficient * (1.0 / totals + moment / (totals * totals))
        + slope_term
    )
    latent_mix = jnp.einsum(
        "uer,zer->uez", weighted_sum_gradient, latent_value_rows, preferred_element_type=jnp.float32
    )
    latent_sgrad = latent_expo * (
        latent_mix + shift_term[..., None] + slope_term[..., None] * latent_score
    )
    latent_residual_gradient = (latent_sgrad * score_scale).astype(jnp.bfloat16)
    query_part = jnp.einsum(
        "nwr,rwb->nwb",
        latent_residual_gradient,
        latent_key_rows,
        preferred_element_type=jnp.float32,
    )
    own_key_grad = (
        jnp.einsum(
            "zry,zrj->yrj",
            latent_residual_gradient,
            query_head_count,
            preferred_element_type=jnp.float32,
        )
        .astype(jnp.bfloat16)
        .reshape(latent_rows, model_width)
    )
    own_value_grad = (
        jnp.einsum(
            "zry,zrj->yrj",
            latent_reduced_precision,
            weighted_sum_gradient,
            preferred_element_type=jnp.float32,
        )
        .astype(jnp.bfloat16)
        .reshape(latent_rows, model_width)
    )
    grad_table = lax.all_gather(
        weighted_sum_gradient.reshape(latent_rows, model_width), "gx", axis=0, tiled=True
    )
    shift_table, slope_table = (
        lax.all_gather(shift_term, "gx", axis=0, tiled=True),
        lax.all_gather(slope_term, "gx", axis=0, tiled=True),
    )
    picked_grad = grad_table.reshape(-1, latent_rows, H, head_size)[item_index]
    picked_shift = shift_table.reshape(-1, latent_rows, H)[item_index]
    picked_slope = slope_table.reshape(-1, latent_rows, H)[item_index]
    media_mix = jnp.einsum(
        "flhd,fphd->flhp", picked_grad, value_heads, preferred_element_type=jnp.float32
    )
    media_sgrad = media_expo * (
        media_mix + picked_shift[..., None] + picked_slope[..., None] * media_score
    )
    media_rgrad = (media_sgrad * score_scale).astype(jnp.bfloat16)
    query_terms = jnp.einsum(
        "flhp,fphd->flhd", media_rgrad, key_heads, preferred_element_type=jnp.float32
    )
    dense_query = collect(item_onehot, query_terms.reshape(frames, -1)).reshape(-1, model_width)
    got_query = lax.psum_scatter(
        dense_query.astype(jnp.bfloat16), "gx", scatter_dimension=0, tiled=True
    ).astype(jnp.float32)
    media_key_grad = (
        jnp.einsum("flhp,flhd->fphd", media_rgrad, picked, preferred_element_type=jnp.float32)
        .astype(jnp.bfloat16)
        .reshape(-1, model_width)
    )
    media_value_grad = (
        jnp.einsum("flhp,flhd->fphd", expo_low, picked_grad, preferred_element_type=jnp.float32)
        .astype(jnp.bfloat16)
        .reshape(-1, model_width)
    )
    grad_key = inner_first(media_normed, media_key_grad) + inner_first(latent_normed, own_key_grad)
    grad_value = inner_first(media_normed, media_value_grad) + inner_first(
        latent_normed, own_value_grad
    )
    media_normed_grad = inner_last(media_key_grad, back_key) + inner_last(
        media_value_grad, back_value
    )
    media_pull = jax.vjp(layer_norm, media_in, back_media_gain.astype(jnp.float32))[1]
    media_grad, grad_media_gain = media_pull(media_normed_grad)
    frame_sums = jnp.sum(media_grad.reshape(frames, patches, model_width), axis=1)
    grad_time = collect(time_onehot, frame_sums)
    query_grad = (
        (got_query.reshape(latent_rows, H, head_size) + query_part)
        .astype(jnp.bfloat16)
        .reshape(latent_rows, model_width)
    )
    latent_normed_grad = (
        inner_last(query_grad, back_query)
        + inner_last(own_key_grad, back_key)
        + inner_last(own_value_grad, back_value)
    )
    latent_pull = jax.vjp(layer_norm, latent_in, back_latent_gain.astype(jnp.float32))[1]
    latent_part, grad_latent_gain = latent_pull(latent_normed_grad)
    latents_grad = middle_grad + latent_part
    piece_query = lax.all_gather(query_grad, ("gx", "gy"), axis=0, tiled=True)
    piece_middle = lax.all_gather(middle_low, ("gx", "gy"), axis=0, tiled=True)
    piece_up = lax.all_gather(up_grad, ("gx", "gy"), axis=0, tiled=True)
    piece_cot = lax.all_gather(cotangent, ("gx", "gy"), axis=0, tiled=True)
    shard_query = inner_first(owned_latent, piece_query)
    shard_out = inner_first(owned_attn, piece_middle)
    shard_up = inner_first(owned_ffn, piece_up)
    shard_down = inner_first(owned_hidden, piece_cot)
    shard_grads = (
        lax.psum_scatter(grad_key, ("gx", "gy"), scatter_dimension=0, tiled=True),
        lax.psum_scatter(grad_value, ("gx", "gy"), scatter_dimension=0, tiled=True),
        lax.psum_scatter(grad_media_gain, ("gx", "gy"), scatter_dimension=0, tiled=True),
        lax.psum_scatter(grad_latent_gain, ("gx", "gy"), scatter_dimension=0, tiled=True),
        lax.psum_scatter(grad_ffn_gain, ("gx", "gy"), scatter_dimension=0, tiled=True),
        lax.psum_scatter(grad_time, ("gx", "gy"), scatter_dimension=1, tiled=True),
    )
    return (
        new_latents,
        media_grad,
        latents_grad,
        shard_grads[5],
        shard_grads[2],
        shard_grads[3],
        shard_grads[4],
        shard_query,
        shard_grads[0],
        shard_grads[1],
        shard_out,
        shard_up,
        shard_down,
    )


GROUP = 4


def mates_of(z, chip, core):
    mates = []
    for j in range(1, 16):
        there = (4 * z + chip + j) % 16
        mates.append((there // 4, 2 * (there % 4) + core))
    return mates


class GiveBack:
    def __init__(self, wires, up_part, down_part, scratch, up_out, down_out):
        self.wires, self.up_part, self.down_part = wires, up_part, down_part
        self.up_out, self.down_out = up_out, down_out
        self.up_near, self.down_near, self.up_got = scratch
        self.z, self.g, self.chip, self.core = here()
        self.places = up_places(self.z, self.chip)

    def first(self):
        near = (self.z, sibling(self.g))
        theirs = 1 - self.core
        self.up = self.wires.send(self.up_part.at[:, :, theirs], self.up_near, near)
        self.down = self.wires.send(self.down_part.at[theirs], self.down_near, near)

    def columns(self):
        self.up.wait_recv()
        core = self.core

        @pl.loop(0, LINES)
        def _(n):
            for q in range(PLANE):
                self.up_part[n, q, core] = self.up_part[n, q, core] + self.up_near[n, q]

        self.moved = []
        for there, _ in self.places:
            self.moved.append(
                self.wires.send(
                    self.up_part.at[there[0], there[1], core],
                    self.up_got.at[self.z, self.chip],
                    (there[0], 2 * there[1] + core),
                )
            )
        self.up_got[self.z, self.chip] = self.up_part[self.z, self.chip, core]

    def rows(self):
        self.down.wait_recv()
        rows = self.down_out.shape[0] // 8
        core = self.core

        @pl.loop(0, 8)
        def _(n):
            block = pl.ds(pl.multiple_of(n * rows, 8), rows)
            self.down_out[block] = self.down_part[core, block] + self.down_near[block]

    def finish(self):
        for copy in self.moved:
            copy.wait_recv()
        width = self.up_got.shape[-1]
        for n in range(LINES):
            for q in range(PLANE):
                first = (n * PLANE + q) * width
                self.up_out[:, first : first + width] = self.up_got[n, q].astype(F32)


GIVE_SEMS = 17


class Total:
    def __init__(self, wires, mine, out, sums, got):
        self.wires, self.out, self.sums, self.got = wires, out, sums, got
        self.z, self.g, _, _ = here()
        self.source = mine
        self.step = 0

    def push(self):
        sides = [sibling(self.g), along_x(self.g), along_y(self.g)]
        if self.step < 3:
            self.copies = [
                self.wires.send(self.source, self.got.at[self.step], (self.z, sides[self.step]))
            ]
        else:
            self.copies = [
                self.wires.send(self.source, self.got.at[3 + k], device)
                for k, device in enumerate(line_of(self.z, self.g))
            ]

    def pull(self):
        for copy in self.copies:
            copy.wait_recv()
        if self.step < 3:
            self.sums[self.step] = self.source[...] + self.got[self.step]
            self.source = self.sums.at[self.step]
            self.step += 1
        else:
            self.out[...] = self.source[...] + self.got[3] + self.got[4] + self.got[5]


def head_masks(rows, width, head_size):
    lane = lax.broadcasted_iota(jnp.int32, (rows, width), 1)
    return [(lane >= h * head_size) & (lane < (h + 1) * head_size) for h in range(GROUP)]


def stacked(block, masks):
    zero = jnp.zeros_like(block)
    return jnp.concatenate([jnp.where(mask, block, zero) for mask in masks], axis=0)


def unstacked(block, masks):
    rows = block.shape[0] // GROUP
    total = jnp.where(masks[0], block[:rows], 0.0)
    for h in range(1, GROUP):
        total = jnp.where(masks[h], block[h * rows : (h + 1) * rows], total)
    return total


def dot_last(a, b):
    return lax.dot_general(a, b, (((1,), (1,)), ((), ())), preferred_element_type=F32)


def dot_first(a, b):
    return lax.dot_general(a, b, (((0,), (0,)), ((), ())), preferred_element_type=F32)


def spread_heads(columns, first, masks):
    out = jnp.where(masks[0], columns[:, first : first + 1], 0.0)
    for h in range(1, GROUP):
        out = jnp.where(masks[h], columns[:, first + h : first + h + 1], out)
    return out


def attend(queries, keys, values, valid, scale, masks):
    rows = queries.shape[0]
    score = dot_last(stacked(queries, masks), keys) * scale
    expo = jnp.exp(score)
    if valid is not None:
        expo = jnp.where(valid > 0, expo, 0.0)
    totals = jnp.sum(expo, axis=1, keepdims=True)
    moments = jnp.sum(expo * score, axis=1, keepdims=True)
    weighted = jnp.dot(expo.astype(BF16), values, preferred_element_type=F32)
    heads = [(totals[h * rows : (h + 1) * rows], moments[h * rows : (h + 1) * rows]) for h in range(GROUP)]
    return unstacked(weighted, masks), heads


def put_heads(heads, group, lane):
    out = jnp.zeros(lane.shape, F32)
    for h, (total, moment) in enumerate(heads):
        out = jnp.where(lane == group * GROUP + h, total, out)
        out = jnp.where(lane == H + group * GROUP + h, moment, out)
    return out


def assemble(smalls, out):
    count, rows, lanes = smalls.shape
    shard = out.shape[1] // count
    block = 8
    row = lax.broadcasted_iota(jnp.int32, (block * lanes, block * shard), 0)
    col = lax.broadcasted_iota(jnp.int32, (block * lanes, block * shard), 1)
    lane = row % lanes
    chosen = ((row // lanes) * shard + lane == col) & (lane < shard)
    place = jnp.where(chosen, 1.0, 0.0).astype(BF16)
    for n in range(count // block):
        pieces = jnp.concatenate([smalls[n * block + d] for d in range(block)], axis=1)
        out[:, n * block * shard : (n + 1) * block * shard] = jnp.dot(
            pieces.astype(BF16), place, preferred_element_type=F32
        )


def up_places(z, chip):
    places = []
    for dz in range(LINES):
        for dx, dy in ((0, 0), (1, 0), (0, 1), (1, 1)):
            if dz or dx or dy:
                x, y = chip % 2, chip // 2
                there = (y + dy) % 2 * 2 + (x + dx) % 2
                places.append(((turn(z, dz), there), (turn(z, LINES - dz) if dz else z, there)))
    return places


def shares(counts_ref, z, g, frame, frames, items):
    position = z * frames + frame
    end, slot = 0, 0
    for item in range(items):
        end = end + counts_ref[g, item]
        slot = slot + jnp.where(end <= position, 1, 0)
    return [jnp.where(slot == item, 1.0, 0.0) for item in range(items)]


def put_times(out, tables, times_ref, frames):
    for frame in range(frames):
        row = jnp.zeros((1, out.shape[1]), F32)
        for t in range(8):
            row = row + jnp.where(times_ref[frame] == t, 1.0, 0.0) * tables[t : t + 1]
        out[frame : frame + 1] = row


def opening_kernel(scale, *refs):
    (
        time_table_ref,
        media_gain_ref,
        latent_gain_ref,
        ffn_gain_ref,
        key_shard,
        value_shard,
        query_shard,
        out_shard,
        latents_ref,
        up_ref,
        down_ref,
        cot_ref,
        media_ref,
        valid_ref,
        counts_ref,
        times_ref,
        tables_out,
        counts_out,
        key_weight_out,
        value_weight_out,
        query_weight_out,
        out_weight_out,
        up_out,
        down_out,
        cot_out,
        normed_out,
        keys_out,
        values_out,
        table_out,
        line_normed_out,
        got_weighted,
        got_stats,
        own_weighted,
        own_stats,
        send_sems,
        recv_sems,
        local_sems,
        up_own,
        small_ref,
        smalls,
        key_weight,
        value_weight,
        query_weight,
        line_latents,
        line_normed,
        normed,
        keys,
        values,
        own_table,
        table,
        time_rows,
        sums,
        weighted,
        stats,
    ) = refs
    z, g, chip, core = here()
    here_chip = 4 * z + chip
    me = 2 * here_chip + core
    items, rows, width = line_latents.shape
    frames, _, patches = valid_ref.shape
    shard = key_shard.shape[0]
    span = width // (H // GROUP)
    up_width = up_out.shape[-1]
    near = (z, sibling(g))
    places = up_places(z, chip)
    greet([(there[0], 2 * there[1] + core) for there, _ in places] + [near])
    wires = Wires(send_sems, recv_sems)
    masks = head_masks(rows, span, span // GROUP)
    lane = lax.broadcasted_iota(jnp.int32, (rows, 128), 1)
    local = []
    small_ref[...] = jnp.zeros_like(small_ref)
    for place, source in (
        (slice(0, 8), time_table_ref),
        (slice(8, 9), media_gain_ref),
        (slice(9, 10), latent_gain_ref),
        (slice(10, 11), ffn_gain_ref),
    ):
        small_ref[place, :shard] = source[...].astype(F32)
    found = valid_ref[0].astype(F32)
    for n in range(1, frames):
        found = found + valid_ref[n].astype(F32)
    small_ref[11:12] = jnp.sum(found, axis=1, keepdims=True) + jnp.zeros((1, 128), F32)

    def keep(source, target):
        copy = pltpu.make_async_copy(source, target, local_sems.at[len(local)])
        copy.start()
        local.append(copy)
        return copy

    def rows_of(ref):
        return lambda zz, gg: ref.at[pl.ds(pl.multiple_of((zz * 8 + gg) * shard, 16), shard)]

    def piece(place):
        return up_ref.at[:, pl.ds(pl.multiple_of((4 * place[0] + place[1]) * up_width, 128), up_width)]

    def whole(source, slot):
        return Spread(wires, source, slot, columns_half, True), keep(source, slot(z, g))

    def small_slot(zz, gg):
        return smalls.at[zz * 8 + gg]

    small = Spread(wires, small_ref, small_slot, rows_half, True)
    small_kept = keep(small_ref, small_slot(z, g))
    key, key_kept = whole(key_shard, rows_of(key_weight))
    value, value_kept = whole(value_shard, rows_of(value_weight))
    query = Spread(wires, query_shard, rows_of(query_weight), rows_parts, True, True)
    query_kept = keep(piece_of(query_shard, z), rows_of(query_weight)(z, g))
    query_line = Line(wires, own_table, lambda zz: table.at[zz])
    out, out_kept = whole(out_shard, rows_of(out_weight_out))
    cot = Spread(wires, cot_ref, lambda zz, gg: cot_out.at[zz * 4 + gg // 2], columns_half, False)
    line = Line(wires, latents_ref, lambda zz: line_latents.at[zz])
    exchange = Exchange(
        wires,
        [(weighted, got_weighted), (stats, got_stats)],
    )
    line_kept = keep(latents_ref, line_latents.at[z])
    up_load = keep(piece((z, chip)), up_own)
    late = [
        out_kept,
        keep(cot_ref, cot_out.at[here_chip]),
        keep(down_ref, down_out.at[core]),
    ]
    prompt = len(local)
    moved, given, down = [], [], []
    chunk = 32

    def normalise(first, last):
        @pl.loop(first, last)
        def _(n):
            block = pl.ds(pl.multiple_of(n * chunk, chunk), chunk)
            frame = n // (patches // chunk)
            row = media_ref[block].astype(F32) + time_rows[pl.ds(frame, 1)]
            normed[block] = layer_norm(row, tables_out[8:9]).astype(BF16)

    def normalise_latents():
        gain = tables_out[9:10]
        line_kept.wait()
        for item in range(items):

            @pl.loop(0, rows // chunk)
            def _(n):
                block = pl.ds(pl.multiple_of(n * chunk, chunk), chunk)
                row = line_latents[item, block].astype(F32)
                line_normed[item, block] = layer_norm(row, gain).astype(BF16)

        normed[frames * patches :] = line_normed[z]

    def tabulate():
        small_kept.wait()
        assemble(smalls, tables_out)
        counts = smalls[0, 8:]
        for n in range(1, smalls.shape[0]):
            counts = counts + smalls[n, 8:]
        counts_out[...] = counts
        put_times(time_rows, tables_out, times_ref, frames)

    def project(left, weight, out, first):
        @pl.loop(first, first + 2)
        def _(n):
            cols = pl.ds(pl.multiple_of(n * span, 128), span)
            out[:, cols] = jnp.dot(
                left[...], weight[:, cols], preferred_element_type=F32
            ).astype(BF16)

    def project_keys(first):
        if first == 0:
            key_kept.wait()
            keep(key_weight, key_weight_out)
            keep(normed, normed_out)
        project(normed, key_weight, keys, first)
        if first > 0:
            keep(keys, keys_out)

    def project_values(first):
        if first == 0:
            value_kept.wait()
            keep(value_weight, value_weight_out)
        project(normed, value_weight, values, first)
        if first > 0:
            keep(values, values_out)

    def project_queries():
        query_kept.wait()
        keep(query_weight, query_weight_out)
        for item in range(items):
            own_table[item] = jnp.dot(
                line_normed[item], query_weight[...], preferred_element_type=F32
            ).astype(BF16)
        table[z] = own_table[...]
        query_line.first()

    def attend_own():
        keep(table, table_out)
        keep(line_normed, line_normed_out)
        sums[...] = jnp.zeros_like(sums)
        stats[...] = jnp.zeros_like(stats)
        last = slice(frames * patches, frames * patches + rows)
        own = jnp.zeros((rows, 128), F32)
        for group in range(H // GROUP):
            cols = slice(group * span, (group + 1) * span)
            part, heads = attend(
                table[group, z], keys[last, cols], values[last, cols], None, scale, masks
            )
            own_weighted[:, cols] = part
            own = own + put_heads(heads, group, lane)
        own_stats[...] = own

    def attend_frames(first, last):
        @pl.loop(first, last)
        def _(frame):
            share = shares(counts_ref, z, g, frame, frames, items)
            block = pl.ds(pl.multiple_of(frame * patches, patches), patches)
            valid = valid_ref[frame]
            found = jnp.zeros((rows, 128), F32)
            for group in range(H // GROUP):
                cols = slice(group * span, (group + 1) * span)
                chosen = share[0] * table[group, 0].astype(F32)
                for item in range(1, items):
                    chosen = chosen + share[item] * table[group, item].astype(F32)
                part, heads = attend(
                    chosen.astype(BF16), keys[block, cols], values[block, cols], valid, scale, masks
                )
                found = found + put_heads(heads, group, lane)
                for item in range(items):
                    sums[item, :, cols] += share[item] * part
            for item in range(items):
                stats[item] += share[item] * found

    def down_first():
        down.append(wires.send(down_ref, down_out.at[core], near))

    def up_first():
        up_load.wait()
        keep(up_own, up_out.at[me])
        given.append(wires.send(up_own, up_out.at[me], near))
        for there, _ in places:
            moved.append(
                wires.send(piece(there), up_out.at[me], (there[0], 2 * there[1] + core))
            )

    def up_last():
        for n, (_, origin) in enumerate(places):
            moved[n].wait_recv()
            held = up_out.at[2 * (4 * origin[0] + origin[1]) + core]
            given.append(wires.send(held, held, near))
        for copy in given:
            copy.wait_recv()

    def sums_first():
        weighted[...] = sums[...].astype(BF16)
        exchange.first()

    small.first()
    out.first()
    small.column(0)
    key.first()
    out.column(0)
    query.first()
    small.column(1)
    value.first()
    small.corner_y(1)
    key.corner_x(0)
    key.column(0)
    small.corner_x(2)
    small.column(2)
    key.column(1)
    key.corner_y(0)
    query.column(0)
    line.first()
    value.column(0)
    cot.first()
    small.corner_y(2)
    query.corner_y(0)
    small.corner_x(0)
    out.column(1)
    query.column(1)
    small.corner_x(3)
    small.corner_y(0)
    out.corner_y(0)
    query.corner_x(0)
    value.column(1)
    key.column(2)
    line.take(0)
    small.corner_x(1)
    small.corner_y(3)
    query.corner_y(1)
    query.corner_x(1)
    value.corner_x(1)
    query.corner_x(2)
    out.corner_y(2)
    value.corner_x(2)
    key.corner_x(1)
    query.column(2)
    out.column(2)
    query.corner_y(2)
    value.corner_y(0)
    query.last(1)
    value.corner_y(2)
    small.last(3)
    small.last(0)
    small.last(1)
    key.last(0)
    small.last(2)
    key.corner_y(1)
    query.corner_x(3)
    cot.column(0)
    value.column(2)
    value.last(2)
    small.finish()
    query.corner_y(3)
    key.corner_y(3)
    value.corner_x(0)
    tabulate()
    line.take(1)
    key.corner_x(3)
    key.corner_y(2)
    key.corner_x(2)
    line.take(2)
    value.corner_y(1)
    cot.column(1)
    normalise_latents()
    normalise(0, 8)
    down_first()
    query.last(2)
    query.last(0)
    cot.corner_x(0)
    query.last(3)
    normalise(8, 16)
    value.corner_x(3)
    out.corner_x(1)
    key.last(3)
    value.corner_y(3)
    query.finish()
    project_queries()
    cot.corner_y(1)
    value.last(1)
    key.last(2)
    key.last(1)
    out.corner_x(2)
    out.corner_x(0)
    cot.corner_x(2)
    key.finish()
    out.corner_y(1)
    cot.column(2)
    value.last(0)
    up_first()
    out.corner_x(3)
    value.last(3)
    project_keys(0)
    project_keys(2)
    value.finish()
    cot.corner_x(1)
    query_line.take(0)
    project_values(0)
    out.last(0)
    cot.corner_x(3)
    project_values(2)
    query_line.take(1)
    query_line.take(2)
    down[0].wait_recv()
    attend_own()
    attend_frames(0, 2)
    attend_frames(2, 4)
    sums_first()
    cot.corner_y(2)
    cot.corner_y(0)
    cot.last(0)
    out.last(1)
    out.corner_y(3)
    cot.corner_y(3)
    out.last(3)
    out.last(2)
    cot.last(2)
    up_last()
    cot.last(3)
    out.finish()
    cot.last(1)
    exchange.finish()
    for copy in late + local[prompt:]:
        copy.wait()
    wires.drain()


def opening(scale, small, weights, latents, w_up, w_down, cotangent, media, valid, counts, times):
    rows, width = latents.shape
    shard = weights[0].shape[0]
    up_rows, up_width = w_up.shape
    all_rows = media.shape[0] + rows
    wires = 5 * spread_sems(True) + spread_sems(False) + 2 * LINE_SEMS + 31 + 1 + 2 * LINES
    span = width // LINES
    square = jax.ShapeDtypeStruct((width, width), BF16)
    table = jax.ShapeDtypeStruct((LINES, rows, width), BF16)
    keys = jax.ShapeDtypeStruct((all_rows, width), BF16)
    smem = pl.BlockSpec(memory_space=pltpu.SMEM)
    return pl.pallas_call(
        partial(opening_kernel, scale),
        out_shape=[
            jax.ShapeDtypeStruct((16, width), F32),
            jax.ShapeDtypeStruct((8, 128), F32),
            square,
            square,
            jax.ShapeDtypeStruct((width, span), BF16),
            square,
            jax.ShapeDtypeStruct((32, up_rows, up_width // 16), BF16),
            jax.ShapeDtypeStruct((2,) + w_down.shape, BF16),
            jax.ShapeDtypeStruct((16,) + cotangent.shape, BF16),
            keys,
            keys,
            keys,
            jax.ShapeDtypeStruct((LINES, LINES, rows, span), BF16),
            table,
            table,
            jax.ShapeDtypeStruct((LINES, rows, 128), F32),
            jax.ShapeDtypeStruct((rows, width), F32),
            jax.ShapeDtypeStruct((rows, 128), F32),
        ],
        in_specs=[VMEM] * 8 + [LEFT] * 2 + [VMEM] * 4 + [smem] * 2,
        out_specs=[VMEM] * 2 + [LEFT] * 12 + [VMEM] * 4,
        scratch_shapes=[
            sems(wires),
            sems(wires),
            sems(24),
            pltpu.VMEM((up_rows, up_width // 16), BF16),
            pltpu.VMEM((16, 128), F32),
            pltpu.VMEM((32, 16, 128), F32),
            pltpu.VMEM((width, width), BF16),
            pltpu.VMEM((width, width), BF16),
            pltpu.VMEM((width, span), BF16),
            pltpu.VMEM((LINES, rows, width), BF16),
            pltpu.VMEM((LINES, rows, width), BF16),
            pltpu.VMEM((all_rows, width), BF16),
            pltpu.VMEM((all_rows, width), BF16),
            pltpu.VMEM((all_rows, width), BF16),
            pltpu.VMEM((LINES, rows, span), BF16),
            pltpu.VMEM((LINES, LINES, rows, span), BF16),
            pltpu.VMEM((8, width), F32),
            pltpu.VMEM((LINES, rows, width), F32),
            pltpu.VMEM((LINES, rows, width), BF16),
            pltpu.VMEM((LINES, rows, 128), F32),
        ],
        compiler_params=params(0),
        name="opening",
    )(*small, *weights, latents, w_up, w_down, cotangent, media, valid, counts, times)


def repel(queries, grads, keys, values, valid, shift, slope, scale, masks):
    query_stack = stacked(queries, masks)
    grad_stack = stacked(grads, masks)
    score = dot_last(query_stack, keys) * scale
    expo = jnp.exp(score)
    if valid is not None:
        expo = jnp.where(valid > 0, expo, 0.0)
    mix = dot_last(grad_stack, values)
    raw = (expo * (mix + shift + slope * score) * scale).astype(BF16)
    query_grad = unstacked(jnp.dot(raw, keys, preferred_element_type=F32), masks)
    key_grad = dot_first(raw, query_stack).astype(BF16)
    value_grad = dot_first(expo.astype(BF16), grad_stack).astype(BF16)
    return query_grad, key_grad, value_grad


def stacked_columns(terms, first):
    return jnp.concatenate([terms[:, first + h : first + h + 1] for h in range(GROUP)], axis=0)


def closing_kernel(scale, *refs):
    (
        table_ref,
        grad_ref,
        terms_ref,
        keys_ref,
        values_ref,
        normed_ref,
        valid_ref,
        attn_ref,
        low_ref,
        own_grad_ref,
        own_terms_ref,
        line_normed_ref,
        query_weight_ref,
        key_weight_ref,
        value_weight_ref,
        media_ref,
        tables_ref,
        latents_ref,
        middle_grad_ref,
        ffn_gain_ref,
        counts_ref,
        times_ref,
        media_grad_out,
        latents_grad_out,
        small_out,
        out_out,
        value_out,
        key_out,
        query_out,
        send_sems,
        recv_sems,
        local_sems,
        table,
        grads,
        keys,
        values,
        normed,
        key_grad,
        value_grad,
        weight_a,
        weight_b,
        sums,
        terms_query,
        got_query,
        query_grad,
        got_line,
        media_grad,
        latent_grad,
        small,
        small_sums,
        small_got,
        time_rows_ref,
        part_a,
        part_b,
        part_c,
        part_d,
        query_relay,
        line_relay,
        *fold,
    ) = refs
    z, g, _, core = here()
    items, rows, width = grads.shape
    frames, _, patches = valid_ref.shape
    media_rows = frames * patches
    shard = width // 32
    groups = H // GROUP
    span = width // groups
    masks = head_masks(rows, span, span // GROUP)
    greet(line_of(z, g) + sides_of(z, g, True))
    wires = Wires(send_sems, recv_sems)
    out = Fold(wires, part_a, True, fold[:FOLD], out_out)
    value = Fold(wires, part_b, True, fold[FOLD : 2 * FOLD], value_out)
    key = Fold(wires, part_c, True, fold[2 * FOLD : 3 * FOLD], key_out)
    query = FoldSplit(wires, part_d, True, fold[3 * FOLD :], query_out)
    total = Total(wires, small, small_out, small_sums, small_got)
    exchange = SumLine(wires, terms_query, got_query, query_relay)
    line_exchange = SumLine(wires, grads, got_line, line_relay)
    local = []

    def load(source, target):
        copy = pltpu.make_async_copy(source, target, local_sems.at[len(local)])
        copy.start()
        local.append(copy)
        return copy

    loads = [
        load(table_ref, table),
        load(grad_ref, grads),
        load(keys_ref, keys),
        load(values_ref, values),
    ]
    normed_load = load(normed_ref, normed)
    key_load = load(key_weight_ref, weight_a)
    value_load = load(value_weight_ref, weight_b)
    stored = []

    def weight_part(part, left, right, first, last):
        @pl.loop(first, last)
        def _(n):
            cols = pl.ds(pl.multiple_of(n * span, 128), span)
            block = dot_first(left[:, cols], right[...]).astype(BF16)
            part[n] = block.reshape(PLANE, 2, shard, width)

    def out_part():
        weight_part(part_a, attn_ref, low_ref, 0, LINES)
        out.start()

    def value_part(first):
        if first == 0:
            normed_load.wait()
        weight_part(part_b, normed, value_grad, first, first + 2)
        if first > 0:
            value.start()

    def key_part(first):
        weight_part(part_c, normed, key_grad, first, first + 2)
        if first > 0:
            key.start()

    def repel_own():
        for copy in loads:
            copy.wait()
        sums[...] = jnp.zeros_like(sums)
        own_terms = own_terms_ref[...]
        for group in range(groups):
            cols = slice(group * span, (group + 1) * span)
            (
                sums[group, z],
                key_grad[media_rows:, cols],
                value_grad[media_rows:, cols],
            ) = repel(
                table[group, z],
                own_grad_ref[:, cols],
                keys[media_rows:, cols],
                values[media_rows:, cols],
                None,
                stacked_columns(own_terms, group * GROUP),
                stacked_columns(own_terms, H + group * GROUP),
                scale,
                masks,
            )

    def repel_frames(first, last):
        @pl.loop(first, last)
        def _(frame):
            block = pl.ds(pl.multiple_of(frame * patches, patches), patches)
            valid = valid_ref[frame]
            share = shares(counts_ref, z, g, frame, frames, items)

            def pick(ref, cols):
                chosen = share[0] * ref[0, :, cols].astype(F32)
                for item in range(1, items):
                    chosen = chosen + share[item] * ref[item, :, cols].astype(F32)
                return chosen

            everything = slice(None)
            terms = pick(terms_ref, everything)
            for group in range(groups):
                cols = slice(group * span, (group + 1) * span)
                query_part, key_grad[block, cols], value_grad[block, cols] = repel(
                    pick(table.at[group], everything).astype(BF16),
                    pick(grads, cols).astype(BF16),
                    keys[block, cols],
                    values[block, cols],
                    valid,
                    stacked_columns(terms, group * GROUP),
                    stacked_columns(terms, H + group * GROUP),
                    scale,
                    masks,
                )
                for item in range(items):
                    sums[group, item] += share[item] * query_part

    def queries_first():
        terms_query[...] = sums[...].astype(BF16)
        exchange.first()

    def media_product(n):
        if n == 0:
            key_load.wait()
            value_load.wait()
            small[...] = jnp.zeros_like(small)
            small[10:11] = ffn_gain_ref[...]
            put_times(time_rows_ref, tables_ref, times_ref, frames)
        if n == 2:
            stored[-1].wait()
        count = media_rows // 2
        block = slice(n // 2 * count, (n // 2 + 1) * count)

        @pl.loop(n % 2 * 2, n % 2 * 2 + 2)
        def _(t):
            cols = pl.ds(pl.multiple_of(t * span, 128), span)
            media_grad[:, cols] = dot_last(key_grad[block], weight_a[cols]) + dot_last(
                value_grad[block], weight_b[cols]
            )

    def media_pull(frame):
        count = media_rows // 2
        gain = tables_ref[8:9]
        chunk = 32
        f = frame % (frames // 2)
        moving = time_rows_ref[frame : frame + 1]

        def step(t, carry):
            gain_sum, row_sum = carry
            here_rows = pl.ds(pl.multiple_of(f * patches + t * chunk, chunk), chunk)
            there_rows = pl.ds(pl.multiple_of(frame * patches + t * chunk, chunk), chunk)
            row = media_ref[there_rows].astype(F32) + moving
            pulled, summand = norm_pull(row, gain, media_grad[here_rows])
            media_grad[here_rows] = pulled
            return (
                gain_sum + jnp.sum(summand, axis=0, keepdims=True),
                row_sum + jnp.sum(pulled, axis=0, keepdims=True),
            )

        zero = jnp.zeros((1, width), F32)
        gain_sum, row_sum = lax.fori_loop(0, patches // chunk, step, (zero, zero))
        small[8:9] += gain_sum
        for t in range(8):
            small[t : t + 1] += jnp.where(times_ref[frame] == t, 1.0, 0.0) * row_sum
        if f == frames // 2 - 1:
            first = frame // (frames // 2) * count
            stored.append(load(media_grad, media_grad_out.at[pl.ds(first, count)]))

    def latents_side():
        @pl.loop(0, groups)
        def _(t):
            cols = pl.ds(pl.multiple_of(t * span, 128), span)
            latent_grad[:, cols] = dot_last(key_grad[media_rows:], weight_a[cols]) + dot_last(
                value_grad[media_rows:], weight_b[cols]
            )

    def query_part():
        for item in range(items):
            found = got_query[0, item].astype(F32)
            for place in range(1, LINES):
                found = found + got_query[place, item].astype(F32)
            query_grad[item] = found.astype(BF16)
        grads_all = query_grad[...].reshape(items * rows, span)

        @pl.loop(0, LINES)
        def _(n):
            cols = pl.ds(pl.multiple_of(n * span, 128), span)
            left = line_normed_ref[:, :, cols].reshape(items * rows, span)
            block = dot_first(left, grads_all).astype(BF16)
            part_d[n] = block.reshape(PLANE, 2, shard, span)

        query.start()

    def line_first():
        for item in range(items):
            grads[item] = dot_last(query_grad[item], query_weight_ref[...]).astype(BF16)
        line_exchange.first()

    def latents_end():
        for place in range(LINES):
            latent_grad[...] += got_line[place].astype(F32)
        pulled, summand = norm_pull(
            latents_ref[...].astype(F32), tables_ref[9:10], latent_grad[...]
        )
        latents_grad_out[...] = middle_grad_ref[...] + pulled
        small[9:10] = jnp.sum(summand, axis=0, keepdims=True)
        total.push()

    def total_next():
        total.pull()
        total.push()

    out_part()
    repel_own()
    repel_frames(0, 2)
    repel_frames(2, 4)
    queries_first()
    out.corner()
    media_product(0)
    value_part(0)
    value_part(2)
    out.side_x()
    out.side_y()
    key_part(0)
    exchange.relay()
    media_product(1)
    value.corner()
    key_part(2)
    media_pull(0)
    media_pull(1)
    exchange.finish()
    query_part()
    key.corner()
    line_first()
    value.side_x()
    value.side_y()
    key.side_x()
    out.line()
    line_exchange.relay()
    media_product(2)
    media_product(3)
    key.side_y()
    media_pull(2)
    out.relay()
    value.line()
    media_pull(3)
    line_exchange.finish()
    query.corner()
    latents_side()
    value.relay()
    latents_end()
    key.line()
    total_next()
    query.side_x()
    query.side_y()
    total_next()
    key.relay()
    out.finish()
    query.line()
    value.finish()
    total_next()
    query.finish()
    key.finish()
    total.pull()
    stored[1].wait()
    wires.drain()


def closing(scale, *args):
    (table, grads, terms, keys, values, normed) = args[:6]
    media, latents = args[15], args[17]
    span = table.shape[-1]
    rows, width = latents.shape
    shard = width // 32
    wires = 4 * fold_sems(True) + 6 + 2 * LINES
    bf = [
        table.shape,
        grads.shape,
        keys.shape,
        keys.shape,
        keys.shape,
        keys.shape,
        keys.shape,
        (width, width),
        (width, width),
    ]
    part = pltpu.VMEM((LINES, PLANE, 2, shard, width), BF16)
    small = (16, width)
    scratch = [pltpu.VMEM(shape, BF16) for shape in bf] + [
        pltpu.VMEM(table.shape, F32),
        pltpu.VMEM(table.shape, BF16),
        pltpu.VMEM(table.shape, BF16),
        pltpu.VMEM(table.shape[1:], BF16),
        pltpu.VMEM(grads.shape, BF16),
        pltpu.VMEM((media.shape[0] // 2, width), F32),
        pltpu.VMEM((rows, width), F32),
        pltpu.VMEM(small, F32),
        pltpu.VMEM((3,) + small, F32),
        pltpu.VMEM((6,) + small, F32),
        pltpu.VMEM((8, width), F32),
        part,
        part,
        part,
        pltpu.VMEM((LINES, PLANE, 2, shard, span), BF16),
        pltpu.VMEM(table.shape[1:], BF16),
        pltpu.VMEM((rows, width), BF16),
    ]
    scratch += fold_scratch(shard, width, True) * 3 + fold_scratch(shard, span, True, True)
    smem = pl.BlockSpec(memory_space=pltpu.SMEM)
    return pl.pallas_call(
        partial(closing_kernel, scale),
        out_shape=[
            jax.ShapeDtypeStruct(media.shape, F32),
            jax.ShapeDtypeStruct(latents.shape, F32),
            jax.ShapeDtypeStruct(small, F32),
        ]
        + [jax.ShapeDtypeStruct((shard, width), F32)] * 4,
        in_specs=[LEFT, LEFT, VMEM, LEFT, LEFT, LEFT]
        + [VMEM] * 7
        + [LEFT] * 2
        + [VMEM] * 5
        + [smem] * 2,
        out_specs=[LEFT] + [VMEM] * 6,
        scratch_shapes=[sems(wires), sems(wires), sems(12)] + scratch,
        compiler_params=pltpu.CompilerParams(
            collective_id=3, has_side_effects=True, vmem_limit_bytes=67043328
        ),
        name="closing",
    )(*args)


def settle_kernel(
    weighted_ref,
    stats_ref,
    own_weighted_ref,
    own_stats_ref,
    out_ref,
    latents_ref,
    gain_ref,
    attention_ref,
    attn_ref,
    sums_ref,
    middle_ref,
    normed_ref,
    ready,
):
    rows, width = latents_ref.shape
    span = width // (H // GROUP)
    masks = head_masks(rows, span, span // GROUP)
    stats = own_stats_ref[...]
    for n in range(stats_ref.shape[0]):
        stats = stats + stats_ref[n]
    sums_ref[...] = stats
    for group in range(H // GROUP):
        cols = pl.ds(group * span, span)
        weighted = own_weighted_ref[:, cols]
        for n in range(weighted_ref.shape[0]):
            weighted = weighted + weighted_ref[n, :, cols].astype(F32)
        attention = weighted / spread_heads(stats, group * GROUP, masks)
        attention_ref[:, cols] = attention
        attn_ref[:, cols] = attention.astype(BF16)
    ready()
    middle = latents_ref[...].astype(F32) + jnp.dot(
        attn_ref[...], out_ref[...], preferred_element_type=F32
    )
    middle_ref[...] = middle
    normed_ref[...] = layer_norm(middle, gain_ref[...]).astype(BF16)


def norm_pull(rows, gain, grad):
    mean = jnp.mean(rows, axis=-1, keepdims=True)
    centred = rows - mean
    inverse = lax.rsqrt(jnp.mean(centred * centred, axis=-1, keepdims=True) + NORM_STABILIZER)
    xhat = centred * inverse
    t = grad * gain
    pulled = (
        t
        - jnp.mean(t, axis=-1, keepdims=True)
        - xhat * jnp.mean(t * xhat, axis=-1, keepdims=True)
    ) * inverse
    return pulled, grad * xhat


def unsettle_kernel(
    normed_grad_ref,
    middle_ref,
    gain_ref,
    cot_ref,
    out_ref,
    attention_ref,
    stats_ref,
    coef,
    middle_grad_ref,
    low_ref,
    gain_grad_ref,
    weighted_grad_ref,
    terms_ref,
    attn_grad,
):
    rows, width = middle_ref.shape
    span = width // (H // GROUP)
    masks = head_masks(rows, span, span // GROUP)
    pulled, summand = norm_pull(middle_ref[...], gain_ref[...], normed_grad_ref[...])
    gain_grad_ref[...] = jnp.sum(summand, axis=0, keepdims=True)
    middle_grad = cot_ref[...].astype(F32) + pulled
    middle_grad_ref[...] = middle_grad
    low_ref[...] = middle_grad.astype(BF16)
    attn_grad[...] = dot_last(low_ref[...], out_ref[...])
    stats = stats_ref[...]
    lane = lax.broadcasted_iota(jnp.int32, (rows, 128), 1)
    terms = jnp.zeros((rows, 128), F32)
    for group in range(H // GROUP):
        cols = pl.ds(group * span, span)
        grad = attn_grad[:, cols]
        first = group * GROUP
        weighted_grad_ref[:, cols] = (grad / spread_heads(stats, first, masks)).astype(BF16)
        along = grad * attention_ref[:, cols]
        for h in range(GROUP):
            inner = jnp.sum(jnp.where(masks[h], along, 0.0), axis=1, keepdims=True)
            total = stats[:, first + h : first + h + 1]
            moment = stats[:, H + first + h : H + first + h + 1]
            slope = -coef / total
            shift = -inner / total + coef * (1.0 / total + moment / (total * total)) + slope
            terms = jnp.where(lane == first + h, shift, terms)
            terms = jnp.where(lane == H + first + h, slope, terms)
    terms_ref[...] = terms


def gelu_parts(rows):
    below = 0.5 * (1.0 + lax.erf(rows * (0.5**0.5)))
    density = jnp.exp(-0.5 * rows * rows) * ((0.5 / jnp.pi) ** 0.5)
    return rows * below, below + rows * density


def middle_kernel(patches, *refs):
    (
        weighted_ref,
        stats_ref,
        own_weighted_ref,
        own_stats_ref,
        out_weight_ref,
        up_ref,
        down_ref,
        cot_rows_ref,
        latents_ref,
        tables_ref,
        cot_ref,
        counts_ref,
        attn_out,
        low_out,
        middle_grad_out,
        gain_grad_out,
        weighted_grad_out,
        terms_out,
        grad_table_out,
        terms_table_out,
        new_latents_out,
        up_grad_out,
        down_grad_out,
        send_sems,
        recv_sems,
        local_sems,
        out_weight,
        up_cols,
        down_rows,
        cot_rows,
        ffn_rows,
        attention,
        sums,
        middle,
        normed,
        hidden_grad,
        up_grad,
        hidden,
        normed_part,
        down_part,
        up_grad_part,
        down_grad_part,
        up_near,
        down_near,
        up_got,
        normed_grad,
        down_sum,
        attn_grad,
        *fold,
    ) = refs
    z, g, chip, core = here()
    rows, width = latents_ref.shape
    span = up_cols.shape[1]
    shard = width // 32
    block_rows = PLANE * rows
    near = (z, sibling(g))
    gain_ref = tables_ref.at[10:11]
    greet([(there[0], 2 * there[1] + core) for there, _ in up_places(z, chip)] + [near])
    wires = Wires(send_sems, recv_sems)
    gather = Spread(
        wires, normed, lambda zz, gg: ffn_rows.at[zz, gg // 2], columns_half, False
    )
    back = FoldSteps(wires, normed_part, fold[:FOLD], normed_grad)
    down = Fold(wires, down_part, False, fold[FOLD:], down_sum)
    give = GiveBack(
        wires,
        up_grad_part,
        down_grad_part,
        (up_near, down_near, up_got),
        up_grad_out,
        down_grad_out,
    )
    grad_line = Line(wires, weighted_grad_out, lambda zz: grad_table_out.at[zz])
    terms_line = Line(wires, terms_out, lambda zz: terms_table_out.at[zz])
    loads = [
        pltpu.make_async_copy(source, target, local_sems.at[n])
        for n, (source, target) in enumerate(
            (
                (out_weight_ref, out_weight),
                (down_ref, down_rows),
                (cot_rows_ref, cot_rows),
                (up_ref, up_cols),
            )
        )
    ]
    for load in loads:
        load.start()

    def settle():
        settle_kernel(
            weighted_ref,
            stats_ref,
            own_weighted_ref,
            own_stats_ref,
            out_weight,
            latents_ref,
            gain_ref,
            attention,
            attn_out,
            sums,
            middle,
            normed,
            loads[0].wait,
        )
        ffn_rows[z, chip] = normed[...]

    def hidden_back():
        loads[1].wait()
        loads[2].wait()
        loads[3].wait()

        @pl.loop(0, LINES)
        def _(n):
            block = cot_rows[n].reshape(block_rows, width)
            hidden_grad[n] = dot_last(block, down_rows[...])

    def group(n):
        place = gather.zs[n]
        block = ffn_rows[place].reshape(block_rows, width)
        value, slope = gelu_parts(jnp.dot(block, up_cols[...], preferred_element_type=F32))
        hidden[place] = value.astype(BF16)
        grad = (hidden_grad[place] * slope).astype(BF16)
        up_grad[place] = grad
        part = dot_last(grad, up_cols[...]).astype(BF16)
        normed_part[place] = part.reshape(PLANE, rows, width)

    def down_product():
        @pl.loop(0, LINES)
        def _(n):
            part = jnp.dot(hidden[n], down_rows[...], preferred_element_type=F32)
            down_part[n] = part.astype(BF16).reshape(PLANE, rows, width)

    def up_gradient():
        grads = up_grad[...].reshape(LINES * block_rows, span)

        @pl.loop(0, LINES)
        def _(n):
            cols = pl.ds(pl.multiple_of(n * span, 128), span)
            block = ffn_rows[:, :, :, cols].reshape(LINES * block_rows, span)
            part = dot_first(block, grads).astype(BF16)
            up_grad_part[n] = part.reshape(PLANE, 2, shard, span)

    def down_gradient():
        rows_up = hidden[...].reshape(LINES * block_rows, span)

        @pl.loop(0, LINES)
        def _(n):
            cols = pl.ds(pl.multiple_of(n * span, 128), span)
            block = cot_rows[:, :, :, cols].reshape(LINES * block_rows, span)
            part = dot_first(rows_up, block)
            down_grad_part[:, :, cols] = part.reshape(2, span // 2, span)

    def unsettle():
        unsettle_kernel(
            normed_grad,
            middle,
            gain_ref,
            cot_ref,
            out_weight,
            attention,
            sums,
            ENTROPY_WEIGHT * patches / counts_ref[3:4, 0:1],
            middle_grad_out,
            low_out,
            gain_grad_out,
            weighted_grad_out,
            terms_out,
            attn_grad,
        )
        grad_table_out[z] = weighted_grad_out[...]
        terms_table_out[z] = terms_out[...]

    def new_rows():
        new_latents_out[...] = (middle[...] + down_sum[...]).astype(BF16)

    settle()
    gather.first()
    gather.column(0)
    gather.column(1)
    gather.corner_x(1)
    gather.corner_y(0)
    gather.corner_x(0)
    gather.corner_y(1)
    gather.column(2)
    gather.last(0)
    gather.corner_x(2)
    hidden_back()
    gather.last(1)
    gather.corner_y(2)
    gather.corner_x(3)
    gather.corner_y(3)
    group(0)
    back.corner(0)
    group(1)
    back.corner(1)
    gather.last(2)
    group(2)
    gather.last(3)
    back.corner(2)
    group(3)
    back.corner(3)
    down_product()
    back.side_y(1)
    back.side_x(1)
    back.side_y(3)
    back.side_x(3)
    back.line(1)
    back.side_y(2)
    back.side_x(2)
    down.start()
    back.side_y(0)
    back.side_x(0)
    back.line(3)
    up_gradient()
    back.line(2)
    down.corner()
    down_gradient()
    back.line(0)
    back.relay()
    give.first()
    give.columns()
    down.side_x()
    back.finish()
    give.rows()
    down.side_y()
    unsettle()
    terms_line.first()
    grad_line.first()
    down.line()
    grad_line.take(0)
    grad_line.take(1)
    grad_line.take(2)
    down.relay()
    terms_line.take(0)
    terms_line.take(1)
    terms_line.take(2)
    give.finish()
    down.finish()
    new_rows()
    wires.drain()


def middle_part(
    patches,
    weighted,
    stats,
    own_weighted,
    own_stats,
    w_out,
    up_cols,
    down_rows,
    cot_rows,
    latents,
    tables,
    cot,
    counts,
):
    rows, width = latents.shape
    span = up_cols.shape[1]
    shard = width // 32
    plane = (LINES, PLANE, rows, width)
    block = (LINES, PLANE * rows, span)
    wires = spread_sems(False) + STEP_SEMS + fold_sems(False) + GIVE_SEMS + 2 * LINE_SEMS
    own = (rows, width)
    terms = own_stats.shape
    bf = [
        w_out.shape,
        up_cols.shape,
        down_rows.shape,
        plane,
        plane,
    ]
    scratch = [pltpu.VMEM(shape, BF16) for shape in bf] + [
        pltpu.VMEM(own, F32),
        pltpu.VMEM(terms, F32),
        pltpu.VMEM(own, F32),
        pltpu.VMEM(own, BF16),
        pltpu.VMEM(block, F32),
        pltpu.VMEM(block, BF16),
        pltpu.VMEM(block, BF16),
        pltpu.VMEM(plane, BF16),
        pltpu.VMEM(plane, BF16),
        pltpu.VMEM((LINES, PLANE, 2, shard, span), BF16),
        pltpu.VMEM((2, span // 2, width), F32),
        pltpu.VMEM((LINES, PLANE, shard, span), BF16),
        pltpu.VMEM((span // 2, width), F32),
        pltpu.VMEM((LINES, PLANE, shard, span), BF16),
        pltpu.VMEM(own, F32),
        pltpu.VMEM(own, F32),
        pltpu.VMEM(own, F32),
    ]
    scratch += fold_scratch(rows, width, False) * 2
    return pl.pallas_call(
        partial(middle_kernel, patches),
        out_shape=[
            jax.ShapeDtypeStruct(own, BF16),
            jax.ShapeDtypeStruct(own, BF16),
            jax.ShapeDtypeStruct(own, F32),
            jax.ShapeDtypeStruct((1, width), F32),
            jax.ShapeDtypeStruct(own, BF16),
            jax.ShapeDtypeStruct(terms, F32),
            jax.ShapeDtypeStruct((LINES,) + own, BF16),
            jax.ShapeDtypeStruct((LINES,) + terms, F32),
            jax.ShapeDtypeStruct(own, BF16),
            jax.ShapeDtypeStruct((shard, span * 16), F32),
            jax.ShapeDtypeStruct((span // 2, width), F32),
        ],
        in_specs=[VMEM] * 4 + [LEFT] * 4 + [VMEM] * 4,
        out_specs=[VMEM] * 11,
        scratch_shapes=[sems(wires), sems(wires), sems(4)] + scratch,
        compiler_params=params(1),
        name="middle",
    )(
        weighted,
        stats,
        own_weighted,
        own_stats,
        w_out,
        up_cols,
        down_rows,
        cot_rows.reshape(plane),
        latents,
        tables,
        cot,
        counts,
    )


def ending_kernel(shard, *refs):
    count = (len(refs) - 6) // 3
    sources, small = refs[:count], refs[count]
    outs = refs[count + 1 : 2 * count + 1]
    small_outs = refs[2 * count + 1 : 2 * count + 5]
    held, arrive = refs[2 * count + 5 : 3 * count + 5], refs[3 * count + 5]
    loads, stores = [], []
    for n in range(count):
        loads.append(pltpu.make_async_copy(sources[n], held[n], arrive.at[n]))
        stores.append(pltpu.make_async_copy(held[n], outs[n], arrive.at[n]))
        loads[n].start()
    z, g, _, _ = here()
    width = small.shape[1]
    turned = pltpu.roll(small[...], width - (8 * z + g) * shard, 1)
    small_outs[0][...] = turned[:8, :shard]
    for n in range(3):
        small_outs[n + 1][...] = turned[8 + n : 9 + n, :shard]
    for n in range(count):
        loads[n].wait()
        stores[n].start()
    for n in range(count):
        stores[n].wait()


def ending(results, small, shard):
    count = len(results)
    return pl.pallas_call(
        partial(ending_kernel, shard),
        out_shape=[jax.ShapeDtypeStruct(r.shape, r.dtype) for r in results]
        + [jax.ShapeDtypeStruct((8, shard), F32)]
        + [jax.ShapeDtypeStruct((1, shard), F32)] * 3,
        in_specs=[LEFT] * count + [VMEM],
        out_specs=[LEFT] * count + [VMEM] * 4,
        scratch_shapes=[pltpu.VMEM(r.shape, r.dtype) for r in results] + [sems(count)],
        name="ending",
    )(*results, small)


def per_device(
    media,
    latents,
    frame_counts,
    time_index,
    valid,
    time_table,
    media_gain,
    latent_gain,
    ffn_gain,
    w_query,
    w_key,
    w_value,
    w_out,
    w_up,
    w_down,
    cotangent,
):
    frames = time_index.shape[0]
    patches = valid.shape[0] // frames
    width = latents.shape[1]
    shard = media_gain.shape[0]
    scale = (width // H) ** (-0.5)
    valid_rows = valid.reshape(frames, 1, patches)
    (
        tables,
        counts,
        full_key,
        full_value,
        full_query,
        full_out,
        up_cols,
        down_rows,
        cot_rows,
        normed,
        keys,
        values,
        table,
        line_normed,
        got_weighted,
        got_stats,
        own_weighted,
        own_stats,
    ) = opening(
        scale,
        (
            time_table,
            media_gain.reshape(1, shard),
            latent_gain.reshape(1, shard),
            ffn_gain.reshape(1, shard),
        ),
        (w_key, w_value, w_query, w_out),
        latents,
        w_up,
        w_down,
        cotangent,
        media,
        valid_rows,
        frame_counts,
        time_index,
    )
    (
        attn_low,
        middle_low,
        middle_grad,
        grad_ffn_gain,
        weighted_grad,
        terms,
        grad_table,
        terms_table,
        new_latents,
        shard_up,
        shard_down,
    ) = middle_part(
        valid.shape[0] * lax.axis_size(AXES),
        got_weighted,
        got_stats,
        own_weighted,
        own_stats,
        full_out,
        up_cols.reshape(width, -1),
        down_rows.reshape(-1, width),
        cot_rows,
        latents,
        tables,
        cotangent,
        counts,
    )
    (
        media_grad,
        latents_grad,
        smalls_grad,
        shard_out,
        shard_value,
        shard_key,
        shard_query,
    ) = closing(
        scale,
        table,
        grad_table,
        terms_table,
        keys,
        values,
        normed,
        valid_rows,
        attn_low,
        middle_low,
        weighted_grad,
        terms,
        line_normed,
        full_query,
        full_key,
        full_value,
        media,
        tables,
        latents,
        middle_grad,
        grad_ffn_gain,
        frame_counts,
        time_index,
    )
    results = ending(
        (
            new_latents,
            media_grad,
            latents_grad,
            shard_query,
            shard_key,
            shard_value,
            shard_out,
            shard_up,
            shard_down,
        ),
        smalls_grad,
        shard,
    )
    time_grad, *gains = results[9:]
    return (
        *results[:3],
        time_grad,
        *(gain.reshape(shard) for gain in gains),
        *results[3:9],
    )


def solution(mesh):
    in_specs = (
        P(("gx", "gy"), None),
        P(("gx", "gy"), None),
        P(),
        P(("gx", "gy")),
        P(("gx", "gy")),
        P(None, ("gx", "gy")),
        P(("gx", "gy")),
        P(("gx", "gy")),
        P(("gx", "gy")),
        P(("gx", "gy"), None),
        P(("gx", "gy"), None),
        P(("gx", "gy"), None),
        P(("gx", "gy"), None),
        P(("gx", "gy"), None),
        P(("gx", "gy"), None),
        P(("gx", "gy"), None),
    )
    out_specs = (
        P(("gx", "gy"), None),
        P(("gx", "gy"), None),
        P(("gx", "gy"), None),
        P(None, ("gx", "gy")),
        P(("gx", "gy")),
        P(("gx", "gy")),
        P(("gx", "gy")),
        P(("gx", "gy"), None),
        P(("gx", "gy"), None),
        P(("gx", "gy"), None),
        P(("gx", "gy"), None),
        P(("gx", "gy"), None),
        P(("gx", "gy"), None),
    )
    return jax.shard_map(
        per_device if dict(mesh.shape) == {"gx": 4, "gy": 8} else plain_device,
        mesh=mesh, in_specs=in_specs, out_specs=out_specs, check_vma=False
    )
```

profile of v0, /device:TPU:0, one launch (start us, length us, event | category | flops | bytes accessed | tf_op | source)
XLA Modules:
  0.0 361.1 jit_solution(10486139268145503674)
XLA Ops:
  0.6 1.3 copy.29.refs_14_.refs_20_
  2.0 142.1 %opening.1 = (f32[16,1536]{1,0:T(8,128)}, f32[8,128]{1,0:T(8,128)}, bf16[1536,1536]{1,0:T(8,128)(2,1)}, bf16[1536,1536]{1,0:T(8,128)(2,1)}, bf16[1536,384]{1,0:T...) custom-call(bf16[8,48]{1,0:T(8,128)(2,1)} %refs_0_.1, ...), custom_call_target="tpu_custom_call" | custom-call | tf_op jit(solution)/shard_map/opening/pallas_call | solution.py:1522
  144.1 114.5 %middle.1 = (bf16[64,1536]{1,0:T(8,128)(2,1)}, bf16[64,1536]{1,0:T(8,128)(2,1)}, f32[64,1536]{1,0:T(8,128)}, f32[1,1536]{1,0:T(1,128)}, bf16[64,1536]{1,0:T(8,12...) custom-call(bf16[4,64,1536]{2,1,0:T(8,128)(2,1)} %get-tuple-element., ...), custom_call_target="tpu_custom_call" | custom-call | tf_op jit(solution)/shard_map/middle/pallas_call | solution.py:2378
  258.6 95.7 %closing.1 = (f32[512,1536]{1,0:T(8,128)}, f32[64,1536]{1,0:T(8,128)}, f32[16,1536]{1,0:T(8,128)}, f32[48,1536]{1,0:T(8,128)}, f32[48,1536]{1,0:T(8,128)}, /*index=5*/f32[48,1536]{1,0:T(8,128)}, f32[48,1536]{1,0:T(8,128)}) custom-call(bf16[4,4,64,384]{3,2,1,0:T(8,128)(2,1)} %get-tuple-element.73.refs_0_, bf16[4,64,1536]{2,1,0:T(8,128)(2,1)} %get-tuple-element.74.refs_1_, ...), custom_call_target="tpu_custom_call" | custom-call | tf_op jit(solution)/shard_map/closing/pallas_call | solution.py:1959
  354.3 6.6 %ending.1 = (bf16[64,1536]{1,0:T(8,128)(2,1)}, f32[512,1536]{1,0:T(8,128)}, f32[64,1536]{1,0:T(8,128)}, f32[48,1536]{1,0:T(8,128)}, f32[48,1536]{1,0:T(8,128)}, ...) custom-call(bf16[64,1536]{1,0:T(8,128)(2,1)} %get-tuple-element.72.r, ...), custom_call_target="tpu_custom_call" | custom-call | tf_op jit(solution)/shard_map/ending/pallas_call | solution.py:2440
where the time goes:
time: 361 us
  Pallas kernels  359 us (99%)
    pallas_call x1, Pallas kernels, opening(): pl.pallas_call(partial(opening_kernel, scale), out_shape=[jax.ShapeDtypeS...  142 us
    pallas_call x1, Pallas kernels, middle_part(): pl.pallas_call(partial(middle_kernel, patches), out_shape=[jax.ShapeDtype...  114 us
    pallas_call x1, Pallas kernels, closing(): pl.pallas_call(partial(closing_kernel, scale), out_shape=[jax.ShapeDtypeS...  95.7 us

commit v1 on v0

--- a/solution.py
+++ b/solution.py
@@ -1069,6 +1069,19 @@
     weighted = jnp.dot(expo.astype(BF16), values, preferred_element_type=F32)
     heads = [(totals[h * rows : (h + 1) * rows], moments[h * rows : (h + 1) * rows]) for h in range(GROUP)]
     return unstacked(weighted, masks), heads
+
+
+def pack_rows(terms):
+    part = terms.shape[0] // 4
+    out = terms[:part]
+    for k in range(1, 4):
+        out = out + pltpu.roll(terms[k * part : (k + 1) * part], 32 * k, 1)
+    return out
+
+
+def unpack_rows(packed):
+    turned = [pltpu.roll(packed, 128 - 32 * k, 1) for k in range(1, 4)]
+    return jnp.concatenate([packed] + turned, axis=0)
 
 
 def put_heads(heads, group, lane):
@@ -1179,6 +1192,7 @@
         sums,
         weighted,
         stats,
+        packed,
     ) = refs
     z, g, chip, core = here()
     here_chip = 4 * z + chip
@@ -1238,7 +1252,7 @@
     line = Line(wires, latents_ref, lambda zz: line_latents.at[zz])
     exchange = Exchange(
         wires,
-        [(weighted, got_weighted), (stats, got_stats)],
+        [(weighted, got_weighted), (packed, got_stats)],
     )
     line_kept = keep(latents_ref, line_latents.at[z])
     up_load = keep(piece((z, chip)), up_own)
@@ -1375,134 +1389,136 @@
 
     def sums_first():
         weighted[...] = sums[...].astype(BF16)
+        for item in range(items):
+            packed[item] = pack_rows(stats[item])
         exchange.first()
 
     small.first()
-    out.first()
+    value.first()
+    small.corner_y(0)
     small.column(0)
+    query.first()
+    down_first()
+    small.column(1)
     key.first()
-    out.column(0)
-    query.first()
-    small.column(1)
-    value.first()
-    small.corner_y(1)
-    key.corner_x(0)
-    key.column(0)
+    small.corner_x(1)
+    value.column(0)
+    key.corner_y(0)
+    line.first()
+    small.corner_y(2)
+    query.column(0)
+    value.column(1)
+    query.column(1)
     small.corner_x(2)
     small.column(2)
+    query.corner_y(0)
+    key.column(0)
+    query.corner_y(2)
+    small.corner_y(1)
+    small.corner_x(3)
+    value.corner_y(0)
+    query.corner_x(0)
+    value.corner_x(1)
+    query.corner_y(1)
+    value.corner_x(0)
+    small.corner_x(0)
+    query.corner_x(1)
+    small.corner_y(3)
+    query.column(2)
+    value.corner_y(1)
     key.column(1)
-    key.corner_y(0)
-    query.column(0)
-    line.first()
-    value.column(0)
+    value.corner_x(2)
+    query.corner_x(2)
+    value.column(2)
+    small.last(1)
+    line.take(0)
+    small.last(0)
+    line.take(1)
+    out.first()
+    key.corner_y(1)
+    query.corner_y(3)
+    small.last(3)
+    value.corner_y(2)
+    small.last(2)
+    query.last(1)
+    small.finish()
+    tabulate()
+    query.corner_x(3)
+    key.column(2)
+    value.last(0)
+    normalise(0, 8)
+    key.corner_x(1)
+    query.last(0)
+    query.last(2)
+    value.corner_y(3)
+    normalise(8, 16)
+    line.take(2)
+    query.last(3)
+    key.corner_x(2)
+    value.corner_x(3)
+    value.last(1)
+    key.corner_x(0)
     cot.first()
-    small.corner_y(2)
-    query.corner_y(0)
-    small.corner_x(0)
+    key.corner_y(3)
+    down[0].wait_recv()
+    query.finish()
+    normalise_latents()
+    project_queries()
+    value.last(2)
+    key.corner_x(3)
+    value.last(3)
+    key.corner_y(2)
+    out.column(0)
+    value.finish()
+    key.last(1)
     out.column(1)
-    query.column(1)
-    small.corner_x(3)
-    small.corner_y(0)
-    out.corner_y(0)
-    query.corner_x(0)
-    value.column(1)
-    key.column(2)
-    line.take(0)
-    small.corner_x(1)
-    small.corner_y(3)
-    query.corner_y(1)
-    query.corner_x(1)
-    value.corner_x(1)
-    query.corner_x(2)
-    out.corner_y(2)
-    value.corner_x(2)
-    key.corner_x(1)
-    query.column(2)
-    out.column(2)
-    query.corner_y(2)
-    value.corner_y(0)
-    query.last(1)
-    value.corner_y(2)
-    small.last(3)
-    small.last(0)
-    small.last(1)
-    key.last(0)
-    small.last(2)
-    key.corner_y(1)
-    query.corner_x(3)
-    cot.column(0)
-    value.column(2)
-    value.last(2)
-    small.finish()
-    query.corner_y(3)
-    key.corner_y(3)
-    value.corner_x(0)
-    tabulate()
-    line.take(1)
-    key.corner_x(3)
-    key.corner_y(2)
-    key.corner_x(2)
-    line.take(2)
-    value.corner_y(1)
-    cot.column(1)
-    normalise_latents()
-    normalise(0, 8)
-    down_first()
-    query.last(2)
-    query.last(0)
-    cot.corner_x(0)
-    query.last(3)
-    normalise(8, 16)
-    value.corner_x(3)
     out.corner_x(1)
     key.last(3)
-    value.corner_y(3)
-    query.finish()
-    project_queries()
-    cot.corner_y(1)
-    value.last(1)
+    key.last(0)
+    out.corner_y(0)
+    cot.corner_x(0)
+    out.column(2)
+    cot.corner_y(0)
     key.last(2)
-    key.last(1)
-    out.corner_x(2)
-    out.corner_x(0)
-    cot.corner_x(2)
+    project_values(0)
+    project_values(2)
+    up_first()
     key.finish()
+    project_keys(0)
     out.corner_y(1)
-    cot.column(2)
-    value.last(0)
-    up_first()
+    query_line.take(0)
+    out.corner_y(3)
     out.corner_x(3)
-    value.last(3)
-    project_keys(0)
     project_keys(2)
-    value.finish()
-    cot.corner_x(1)
-    query_line.take(0)
-    project_values(0)
-    out.last(0)
-    cot.corner_x(3)
-    project_values(2)
+    cot.last(0)
+    cot.column(0)
     query_line.take(1)
     query_line.take(2)
-    down[0].wait_recv()
+    cot.column(1)
+    out.corner_y(2)
     attend_own()
     attend_frames(0, 2)
+    out.corner_x(2)
     attend_frames(2, 4)
     sums_first()
+    out.corner_x(0)
+    out.last(1)
+    cot.column(2)
     cot.corner_y(2)
-    cot.corner_y(0)
-    cot.last(0)
-    out.last(1)
-    out.corner_y(3)
+    cot.corner_x(1)
+    cot.corner_y(1)
+    cot.corner_x(2)
     cot.corner_y(3)
+    cot.corner_x(3)
     out.last(3)
+    up_last()
+    out.last(0)
     out.last(2)
+    out.finish()
+    exchange.finish()
     cot.last(2)
-    up_last()
     cot.last(3)
-    out.finish()
     cot.last(1)
-    exchange.finish()
     for copy in late + local[prompt:]:
         copy.wait()
     wires.drain()
@@ -1537,7 +1553,7 @@
             jax.ShapeDtypeStruct((LINES, LINES, rows, span), BF16),
             table,
             table,
-            jax.ShapeDtypeStruct((LINES, rows, 128), F32),
+            jax.ShapeDtypeStruct((LINES, rows // 4, 128), F32),
             jax.ShapeDtypeStruct((rows, width), F32),
             jax.ShapeDtypeStruct((rows, 128), F32),
         ],
@@ -1564,6 +1580,7 @@
             pltpu.VMEM((LINES, rows, width), F32),
             pltpu.VMEM((LINES, rows, width), BF16),
             pltpu.VMEM((LINES, rows, 128), F32),
+            pltpu.VMEM((LINES, rows // 4, 128), F32),
         ],
         compiler_params=params(0),
         name="opening",
@@ -1747,7 +1764,7 @@
                 return chosen
 
             everything = slice(None)
-            terms = pick(terms_ref, everything)
+            terms = unpack_rows(pick(terms_ref, everything))
             for group in range(groups):
                 cols = slice(group * span, (group + 1) * span)
                 query_part, key_grad[block, cols], value_grad[block, cols] = repel(
@@ -1996,9 +2013,10 @@
     rows, width = latents_ref.shape
     span = width // (H // GROUP)
     masks = head_masks(rows, span, span // GROUP)
-    stats = own_stats_ref[...]
-    for n in range(stats_ref.shape[0]):
-        stats = stats + stats_ref[n]
+    found = stats_ref[0]
+    for n in range(1, stats_ref.shape[0]):
+        found = found + stats_ref[n]
+    stats = own_stats_ref[...] + unpack_rows(found)
     sums_ref[...] = stats
     for group in range(H // GROUP):
         cols = pl.ds(group * span, span)
@@ -2131,6 +2149,7 @@
         normed_grad,
         down_sum,
         attn_grad,
+        packed,
         *fold,
     ) = refs
     z, g, chip, core = here()
@@ -2156,7 +2175,7 @@
         down_grad_out,
     )
     grad_line = Line(wires, weighted_grad_out, lambda zz: grad_table_out.at[zz])
-    terms_line = Line(wires, terms_out, lambda zz: terms_table_out.at[zz])
+    terms_line = Line(wires, packed, lambda zz: terms_table_out.at[zz])
     loads = [
         pltpu.make_async_copy(source, target, local_sems.at[n])
         for n, (source, target) in enumerate(
@@ -2253,7 +2272,8 @@
             attn_grad,
         )
         grad_table_out[z] = weighted_grad_out[...]
-        terms_table_out[z] = terms_out[...]
+        packed[...] = pack_rows(terms_out[...])
+        terms_table_out[z] = packed[...]
 
     def new_rows():
         new_latents_out[...] = (middle[...] + down_sum[...]).astype(BF16)
@@ -2262,64 +2282,64 @@
     gather.first()
     gather.column(0)
     gather.column(1)
+    gather.corner_y(0)
     gather.corner_x(1)
-    gather.corner_y(0)
     gather.corner_x(0)
     gather.corner_y(1)
     gather.column(2)
     gather.last(0)
     gather.corner_x(2)
     hidden_back()
-    gather.last(1)
     gather.corner_y(2)
-    gather.corner_x(3)
-    gather.corner_y(3)
     group(0)
     back.corner(0)
+    gather.corner_y(3)
+    gather.corner_x(3)
+    gather.last(1)
     group(1)
+    gather.last(2)
     back.corner(1)
-    gather.last(2)
     group(2)
+    back.corner(2)
     gather.last(3)
-    back.corner(2)
+    back.side_x(0)
     group(3)
     back.corner(3)
+    back.side_y(2)
+    back.side_y(1)
+    up_gradient()
+    back.side_x(2)
     down_product()
-    back.side_y(1)
-    back.side_x(1)
     back.side_y(3)
     back.side_x(3)
-    back.line(1)
-    back.side_y(2)
-    back.side_x(2)
+    back.side_y(0)
+    back.side_x(1)
+    down_gradient()
+    give.first()
     down.start()
-    back.side_y(0)
-    back.side_x(0)
-    back.line(3)
-    up_gradient()
     back.line(2)
     down.corner()
-    down_gradient()
+    back.line(3)
+    give.columns()
+    back.line(1)
     back.line(0)
     back.relay()
-    give.first()
-    give.columns()
     down.side_x()
+    down.side_y()
     back.finish()
-    give.rows()
-    down.side_y()
     unsettle()
+    grad_line.first()
     terms_line.first()
-    grad_line.first()
-    down.line()
     grad_line.take(0)
     grad_line.take(1)
+    down.line()
     grad_line.take(2)
-    down.relay()
     terms_line.take(0)
     terms_line.take(1)
+    give.rows()
+    down.relay()
+    give.finish()
     terms_line.take(2)
-    give.finish()
     down.finish()
     new_rows()
     wires.drain()
@@ -2373,6 +2393,7 @@
         pltpu.VMEM(own, F32),
         pltpu.VMEM(own, F32),
         pltpu.VMEM(own, F32),
+        pltpu.VMEM((rows // 4, 128), F32),
     ]
     scratch += fold_scratch(rows, width, False) * 2
     return pl.pallas_call(
@@ -2385,7 +2406,7 @@
             jax.ShapeDtypeStruct(own, BF16),
             jax.ShapeDtypeStruct(terms, F32),
             jax.ShapeDtypeStruct((LINES,) + own, BF16),
-            jax.ShapeDtypeStruct((LINES,) + terms, F32),
+            jax.ShapeDtypeStruct((LINES, rows // 4, 128), F32),
             jax.ShapeDtypeStruct(own, BF16),
             jax.ShapeDtypeStruct((shard, span * 16), F32),
             jax.ShapeDtypeStruct((span // 2, width), F32),

time: 361 us -> 348 us (0.964)
  Pallas kernels: 359 us -> 346 us
    pallas_call x1, Pallas kernels: 142 us -> 126 us  [opening(): pl.pallas_call(partial(opening_kernel, scale), out_shape=[jax.ShapeDtypeS...]
where the time goes in v1:
time: 348 us
  Pallas kernels  346 us (99%)
    pallas_call x1, Pallas kernels, opening(): pl.pallas_call(partial(opening_kernel, scale), out_shape=[jax.ShapeDtypeS...  126 us
    pallas_call x1, Pallas kernels, middle_part(): pl.pallas_call(partial(middle_kernel, patches), out_shape=[jax.ShapeDtype...  115 us
    pallas_call x1, Pallas kernels, closing(): pl.pallas_call(partial(closing_kernel, scale), out_shape=[jax.ShapeDtypeS...  98.1 us

profile of v1, /device:TPU:0, one launch (start us, length us, event | category | flops | bytes accessed | tf_op | source)
XLA Modules:
  0.0 347.7 jit_solution(16722151616533415457)
XLA Ops:
  0.6 1.3 copy.29.refs_14_.refs_20_
  2.0 126.2 %opening.1 = (f32[16,1536]{1,0:T(8,128)}, f32[8,128]{1,0:T(8,128)}, bf16[1536,1536]{1,0:T(8,128)(2,1)}, bf16[1536,1536]{1,0:T(8,128)(2,1)}, bf16[1536,384]{1,0:T...) custom-call(bf16[8,48]{1,0:T(8,128)(2,1)} %refs_0_.1, ...), custom_call_target="tpu_custom_call" | custom-call | tf_op jit(solution)/shard_map/opening/pallas_call | solution.py:1538
  128.2 114.6 %middle.1 = (bf16[64,1536]{1,0:T(8,128)(2,1)}, bf16[64,1536]{1,0:T(8,128)(2,1)}, f32[64,1536]{1,0:T(8,128)}, f32[1,1536]{1,0:T(1,128)}, bf16[64,1536]{1,0:T(8,12...) custom-call(bf16[4,64,1536]{2,1,0:T(8,128)(2,1)} %get-tuple-element., ...), custom_call_target="tpu_custom_call" | custom-call | tf_op jit(solution)/shard_map/middle/pallas_call | solution.py:2399
  242.9 98.1 %closing.1 = (f32[512,1536]{1,0:T(8,128)}, f32[64,1536]{1,0:T(8,128)}, f32[16,1536]{1,0:T(8,128)}, f32[48,1536]{1,0:T(8,128)}, f32[48,1536]{1,0:T(8,128)}, /*index=5*/f32[48,1536]{1,0:T(8,128)}, f32[48,1536]{1,0:T(8,128)}) custom-call(bf16[4,4,64,384]{3,2,1,0:T(8,128)(2,1)} %get-tuple-element.73.refs_0_, bf16[4,64,1536]{2,1,0:T(8,128)(2,1)} %get-tuple-element.74.refs_1_, ...), custom_call_target="tpu_custom_call" | custom-call | tf_op jit(solution)/shard_map/closing/pallas_call | solution.py:1976
  341.0 6.6 %ending.1 = (bf16[64,1536]{1,0:T(8,128)(2,1)}, f32[512,1536]{1,0:T(8,128)}, f32[64,1536]{1,0:T(8,128)}, f32[48,1536]{1,0:T(8,128)}, f32[48,1536]{1,0:T(8,128)}, ...) custom-call(bf16[64,1536]{1,0:T(8,128)(2,1)} %get-tuple-element.72.r, ...), custom_call_target="tpu_custom_call" | custom-call | tf_op jit(solution)/shard_map/ending/pallas_call | solution.py:2461

commit v2 on v1

--- a/solution.py
+++ b/solution.py
@@ -1394,131 +1394,131 @@
         exchange.first()
 
     small.first()
+    query.first()
     value.first()
+    key.first()
+    query.column(0)
+    small.column(0)
+    small.column(1)
+    small.column(2)
+    query.column(1)
+    down_first()
+    value.column(0)
+    small.corner_x(0)
+    small.corner_y(2)
+    small.corner_y(3)
+    query.corner_y(2)
+    value.column(1)
+    small.corner_x(1)
+    key.column(0)
     small.corner_y(0)
-    small.column(0)
-    query.first()
-    down_first()
-    small.column(1)
-    key.first()
-    small.corner_x(1)
-    value.column(0)
-    key.corner_y(0)
-    line.first()
-    small.corner_y(2)
-    query.column(0)
-    value.column(1)
-    query.column(1)
+    small.corner_y(1)
+    value.corner_x(1)
+    small.corner_x(3)
     small.corner_x(2)
-    small.column(2)
-    query.corner_y(0)
-    key.column(0)
-    query.corner_y(2)
-    small.corner_y(1)
-    small.corner_x(3)
-    value.corner_y(0)
-    query.corner_x(0)
-    value.corner_x(1)
-    query.corner_y(1)
-    value.corner_x(0)
-    small.corner_x(0)
-    query.corner_x(1)
-    small.corner_y(3)
-    query.column(2)
+    value.corner_y(2)
     value.corner_y(1)
     key.column(1)
+    line.first()
+    query.corner_x(0)
+    query.corner_x(2)
+    value.corner_y(0)
+    query.corner_y(0)
+    small.last(1)
+    query.column(2)
+    value.column(2)
+    small.last(3)
+    query.corner_x(1)
+    small.last(0)
+    small.last(2)
+    query.corner_y(1)
+    key.corner_x(2)
+    small.finish()
+    value.corner_x(0)
+    query.corner_x(3)
+    query.corner_y(3)
+    key.corner_x(1)
+    line.take(0)
+    cot.first()
+    tabulate()
+    line.take(1)
+    key.corner_y(1)
+    value.corner_x(3)
     value.corner_x(2)
-    query.corner_x(2)
-    value.column(2)
-    small.last(1)
-    line.take(0)
-    small.last(0)
-    line.take(1)
+    query.last(2)
+    normalise(0, 8)
+    key.corner_y(2)
+    value.last(0)
+    query.last(0)
+    query.last(1)
+    value.corner_y(3)
+    key.column(2)
+    value.last(1)
+    key.corner_y(0)
+    normalise(8, 16)
+    query.last(3)
+    line.take(2)
+    key.corner_x(0)
+    cot.corner_y(0)
+    normalise_latents()
+    cot.column(0)
+    key.last(1)
+    value.last(3)
+    cot.corner_x(0)
+    value.last(2)
+    query.finish()
+    project_queries()
+    value.finish()
+    key.corner_x(3)
+    cot.column(1)
+    project_values(0)
+    key.last(2)
+    key.corner_y(3)
     out.first()
-    key.corner_y(1)
-    query.corner_y(3)
-    small.last(3)
-    value.corner_y(2)
-    small.last(2)
-    query.last(1)
-    small.finish()
-    tabulate()
-    query.corner_x(3)
-    key.column(2)
-    value.last(0)
-    normalise(0, 8)
-    key.corner_x(1)
-    query.last(0)
-    query.last(2)
-    value.corner_y(3)
-    normalise(8, 16)
-    line.take(2)
-    query.last(3)
-    key.corner_x(2)
-    value.corner_x(3)
-    value.last(1)
-    key.corner_x(0)
-    cot.first()
-    key.corner_y(3)
-    down[0].wait_recv()
-    query.finish()
-    normalise_latents()
-    project_queries()
-    value.last(2)
-    key.corner_x(3)
-    value.last(3)
-    key.corner_y(2)
-    out.column(0)
-    value.finish()
-    key.last(1)
-    out.column(1)
-    out.corner_x(1)
+    cot.corner_y(1)
+    up_first()
+    project_values(2)
+    cot.column(2)
+    query_line.take(0)
+    key.last(0)
     key.last(3)
-    key.last(0)
-    out.corner_y(0)
-    cot.corner_x(0)
-    out.column(2)
-    cot.corner_y(0)
-    key.last(2)
-    project_values(0)
-    project_values(2)
-    up_first()
+    cot.corner_x(1)
     key.finish()
     project_keys(0)
-    out.corner_y(1)
-    query_line.take(0)
-    out.corner_y(3)
-    out.corner_x(3)
+    out.column(0)
+    query_line.take(1)
+    out.column(1)
+    out.corner_x(0)
+    cot.last(0)
+    out.corner_y(0)
     project_keys(2)
-    cot.last(0)
-    cot.column(0)
-    query_line.take(1)
     query_line.take(2)
-    cot.column(1)
-    out.corner_y(2)
     attend_own()
     attend_frames(0, 2)
+    attend_frames(2, 4)
+    out.column(2)
+    cot.corner_x(2)
+    out.corner_x(1)
+    out.corner_y(1)
+    cot.corner_y(3)
+    sums_first()
+    cot.corner_x(3)
+    out.corner_y(3)
     out.corner_x(2)
-    attend_frames(2, 4)
-    sums_first()
-    out.corner_x(0)
+    down[0].wait_recv()
+    out.last(0)
+    out.corner_x(3)
+    out.corner_y(2)
+    cot.last(3)
+    up_last()
+    cot.last(1)
+    cot.corner_y(2)
     out.last(1)
-    cot.column(2)
-    cot.corner_y(2)
-    cot.corner_x(1)
-    cot.corner_y(1)
-    cot.corner_x(2)
-    cot.corner_y(3)
-    cot.corner_x(3)
+    out.last(2)
     out.last(3)
-    up_last()
-    out.last(0)
-    out.last(2)
+    cot.last(2)
     out.finish()
     exchange.finish()
-    cot.last(2)
-    cot.last(3)
-    cot.last(1)
     for copy in late + local[prompt:]:
         copy.wait()
     wires.drain()
@@ -1716,8 +1716,6 @@
         out.start()
 
     def value_part(first):
-        if first == 0:
-            normed_load.wait()
         weight_part(part_b, normed, value_grad, first, first + 2)
         if first > 0:
             value.start()
@@ -1730,6 +1728,7 @@
     def repel_own():
         for copy in loads:
             copy.wait()
+        normed_load.wait()
         sums[...] = jnp.zeros_like(sums)
         own_terms = own_terms_ref[...]
         for group in range(groups):
@@ -1880,53 +1879,53 @@
     repel_own()
     repel_frames(0, 2)
     repel_frames(2, 4)
+    out.corner()
     queries_first()
-    out.corner()
     media_product(0)
+    key_part(0)
+    key_part(2)
+    out.side_x()
+    out.side_y()
+    media_product(1)
+    media_pull(0)
+    exchange.relay()
+    key.corner()
     value_part(0)
     value_part(2)
-    out.side_x()
-    out.side_y()
-    key_part(0)
-    exchange.relay()
-    media_product(1)
-    value.corner()
-    key_part(2)
-    media_pull(0)
     media_pull(1)
     exchange.finish()
     query_part()
-    key.corner()
     line_first()
+    value.corner()
+    media_product(2)
+    media_product(3)
+    key.side_x()
+    key.side_y()
+    media_pull(2)
     value.side_x()
-    value.side_y()
-    key.side_x()
     out.line()
     line_exchange.relay()
-    media_product(2)
-    media_product(3)
-    key.side_y()
-    media_pull(2)
+    value.side_y()
+    media_pull(3)
+    key.line()
     out.relay()
-    value.line()
-    media_pull(3)
     line_exchange.finish()
+    key.relay()
     query.corner()
     latents_side()
-    value.relay()
     latents_end()
-    key.line()
+    value.line()
     total_next()
+    out.finish()
     query.side_x()
     query.side_y()
+    key.finish()
+    value.relay()
     total_next()
-    key.relay()
-    out.finish()
     query.line()
-    value.finish()
     total_next()
     query.finish()
-    key.finish()
+    value.finish()
     total.pull()
     stored[1].wait()
     wires.drain()
@@ -2280,66 +2279,66 @@
 
     settle()
     gather.first()
+    gather.corner_x(0)
+    gather.corner_y(0)
     gather.column(0)
     gather.column(1)
-    gather.corner_y(0)
+    hidden_back()
+    gather.last(0)
+    group(0)
+    back.corner(0)
     gather.corner_x(1)
-    gather.corner_x(0)
     gather.corner_y(1)
     gather.column(2)
-    gather.last(0)
     gather.corner_x(2)
-    hidden_back()
     gather.corner_y(2)
-    group(0)
-    back.corner(0)
-    gather.corner_y(3)
-    gather.corner_x(3)
     gather.last(1)
     group(1)
+    back.corner(1)
+    gather.corner_x(3)
+    back.side_y(0)
+    gather.corner_y(3)
+    back.side_x(0)
     gather.last(2)
-    back.corner(1)
     group(2)
     back.corner(2)
     gather.last(3)
-    back.side_x(0)
     group(3)
     back.corner(3)
+    back.side_x(1)
+    back.side_y(1)
+    back.line(0)
+    down_gradient()
+    up_gradient()
+    give.first()
+    back.side_x(2)
     back.side_y(2)
-    back.side_y(1)
-    up_gradient()
-    back.side_x(2)
+    back.side_y(3)
     down_product()
-    back.side_y(3)
+    down.start()
     back.side_x(3)
-    back.side_y(0)
-    back.side_x(1)
-    down_gradient()
-    give.first()
-    down.start()
+    down.corner()
+    give.columns()
     back.line(2)
-    down.corner()
     back.line(3)
-    give.columns()
+    give.rows()
     back.line(1)
-    back.line(0)
-    back.relay()
     down.side_x()
     down.side_y()
+    back.relay()
     back.finish()
     unsettle()
     grad_line.first()
+    grad_line.take(0)
     terms_line.first()
-    grad_line.take(0)
-    grad_line.take(1)
     down.line()
-    grad_line.take(2)
     terms_line.take(0)
     terms_line.take(1)
-    give.rows()
+    grad_line.take(1)
+    grad_line.take(2)
+    terms_line.take(2)
     down.relay()
     give.finish()
-    terms_line.take(2)
     down.finish()
     new_rows()
     wires.drain()

time: 348 us -> 344 us (0.989)
  Pallas kernels: 346 us -> 342 us
    pallas_call x1, Pallas kernels: 126 us -> 123 us  [opening(): pl.pallas_call(partial(opening_kernel, scale), out_shape=[jax.ShapeDtypeS...]
where the time goes in v2:
time: 344 us
  Pallas kernels  342 us (99%)
    pallas_call x1, Pallas kernels, opening(): pl.pallas_call(partial(opening_kernel, scale), out_shape=[jax.ShapeDtypeS...  123 us
    pallas_call x1, Pallas kernels, middle_part(): pl.pallas_call(partial(middle_kernel, patches), out_shape=[jax.ShapeDtype...  116 us
    pallas_call x1, Pallas kernels, closing(): pl.pallas_call(partial(closing_kernel, scale), out_shape=[jax.ShapeDtypeS...  96.7 us

profile of v2, /device:TPU:0, one launch (start us, length us, event | category | flops | bytes accessed | tf_op | source)
XLA Modules:
  0.0 344.2 jit_solution(2497685902980191944)
XLA Ops:
  0.6 1.3 copy.29.refs_14_.refs_20_
  2.0 122.7 %opening.1 = (f32[16,1536]{1,0:T(8,128)}, f32[8,128]{1,0:T(8,128)}, bf16[1536,1536]{1,0:T(8,128)(2,1)}, bf16[1536,1536]{1,0:T(8,128)(2,1)}, bf16[1536,384]{1,0:T...) custom-call(bf16[8,48]{1,0:T(8,128)(2,1)} %refs_0_.1, ...), custom_call_target="tpu_custom_call" | custom-call | tf_op jit(solution)/shard_map/opening/pallas_call | solution.py:1538
  124.7 116.1 %middle.1 = (bf16[64,1536]{1,0:T(8,128)(2,1)}, bf16[64,1536]{1,0:T(8,128)(2,1)}, f32[64,1536]{1,0:T(8,128)}, f32[1,1536]{1,0:T(1,128)}, bf16[64,1536]{1,0:T(8,12...) custom-call(bf16[4,64,1536]{2,1,0:T(8,128)(2,1)} %get-tuple-element., ...), custom_call_target="tpu_custom_call" | custom-call | tf_op jit(solution)/shard_map/middle/pallas_call | solution.py:2398
  240.7 96.7 %closing.1 = (f32[512,1536]{1,0:T(8,128)}, f32[64,1536]{1,0:T(8,128)}, f32[16,1536]{1,0:T(8,128)}, f32[48,1536]{1,0:T(8,128)}, f32[48,1536]{1,0:T(8,128)}, /*index=5*/f32[48,1536]{1,0:T(8,128)}, f32[48,1536]{1,0:T(8,128)}) custom-call(bf16[4,4,64,384]{3,2,1,0:T(8,128)(2,1)} %get-tuple-element.73.refs_0_, bf16[4,64,1536]{2,1,0:T(8,128)(2,1)} %get-tuple-element.74.refs_1_, ...), custom_call_target="tpu_custom_call" | custom-call | tf_op jit(solution)/shard_map/closing/pallas_call | solution.py:1975
  337.5 6.6 %ending.1 = (bf16[64,1536]{1,0:T(8,128)(2,1)}, f32[512,1536]{1,0:T(8,128)}, f32[64,1536]{1,0:T(8,128)}, f32[48,1536]{1,0:T(8,128)}, f32[48,1536]{1,0:T(8,128)}, ...) custom-call(bf16[64,1536]{1,0:T(8,128)(2,1)} %get-tuple-element.72.r, ...), custom_call_target="tpu_custom_call" | custom-call | tf_op jit(solution)/shard_map/ending/pallas_call | solution.py:2460

commit v3 on v2

--- a/solution.py
+++ b/solution.py
@@ -2441,6 +2441,8 @@
     for n in range(count):
         loads.append(pltpu.make_async_copy(sources[n], held[n], arrive.at[n]))
         stores.append(pltpu.make_async_copy(held[n], outs[n], arrive.at[n]))
+    largest = sorted(range(count), key=lambda n: -sources[n].shape[0] * sources[n].shape[1])
+    for n in largest:
         loads[n].start()
     z, g, _, _ = here()
     width = small.shape[1]
@@ -2448,7 +2450,7 @@
     small_outs[0][...] = turned[:8, :shard]
     for n in range(3):
         small_outs[n + 1][...] = turned[8 + n : 9 + n, :shard]
-    for n in range(count):
+    for n in largest:
         loads[n].wait()
         stores[n].start()
     for n in range(count):

time: 344 us -> 344 us (level)
  no operation moved by 1% of the time
where the time goes in v3:
time: 344 us
  Pallas kernels  342 us (99%)
    pallas_call x1, Pallas kernels, opening(): pl.pallas_call(partial(opening_kernel, scale), out_shape=[jax.ShapeDtypeS...  123 us
    pallas_call x1, Pallas kernels, middle_part(): pl.pallas_call(partial(middle_kernel, patches), out_shape=[jax.ShapeDtype...  116 us
    pallas_call x1, Pallas kernels, closing(): pl.pallas_call(partial(closing_kernel, scale), out_shape=[jax.ShapeDtypeS...  96.7 us

profile of v3, /device:TPU:0, one launch (start us, length us, event | category | flops | bytes accessed | tf_op | source)
XLA Modules:
  0.0 344.1 jit_solution(7893049217690335883)
XLA Ops:
  0.6 1.3 copy.29.refs_14_.refs_20_
  2.0 122.7 %opening.1 = (f32[16,1536]{1,0:T(8,128)}, f32[8,128]{1,0:T(8,128)}, bf16[1536,1536]{1,0:T(8,128)(2,1)}, bf16[1536,1536]{1,0:T(8,128)(2,1)}, bf16[1536,384]{1,0:T...) custom-call(bf16[8,48]{1,0:T(8,128)(2,1)} %refs_0_.1, ...), custom_call_target="tpu_custom_call" | custom-call | tf_op jit(solution)/shard_map/opening/pallas_call | solution.py:1538
  124.7 116.1 %middle.1 = (bf16[64,1536]{1,0:T(8,128)(2,1)}, bf16[64,1536]{1,0:T(8,128)(2,1)}, f32[64,1536]{1,0:T(8,128)}, f32[1,1536]{1,0:T(1,128)}, bf16[64,1536]{1,0:T(8,12...) custom-call(bf16[4,64,1536]{2,1,0:T(8,128)(2,1)} %get-tuple-element., ...), custom_call_target="tpu_custom_call" | custom-call | tf_op jit(solution)/shard_map/middle/pallas_call | solution.py:2398
  240.7 96.7 %closing.1 = (f32[512,1536]{1,0:T(8,128)}, f32[64,1536]{1,0:T(8,128)}, f32[16,1536]{1,0:T(8,128)}, f32[48,1536]{1,0:T(8,128)}, f32[48,1536]{1,0:T(8,128)}, /*index=5*/f32[48,1536]{1,0:T(8,128)}, f32[48,1536]{1,0:T(8,128)}) custom-call(bf16[4,4,64,384]{3,2,1,0:T(8,128)(2,1)} %get-tuple-element.73.refs_0_, bf16[4,64,1536]{2,1,0:T(8,128)(2,1)} %get-tuple-element.74.refs_1_, ...), custom_call_target="tpu_custom_call" | custom-call | tf_op jit(solution)/shard_map/closing/pallas_call | solution.py:1975
  337.5 6.4 %ending.1 = (bf16[64,1536]{1,0:T(8,128)(2,1)}, f32[512,1536]{1,0:T(8,128)}, f32[64,1536]{1,0:T(8,128)}, f32[48,1536]{1,0:T(8,128)}, f32[48,1536]{1,0:T(8,128)}, ...) custom-call(bf16[64,1536]{1,0:T(8,128)(2,1)} %get-tuple-element.72.r, ...), custom_call_target="tpu_custom_call" | custom-call | tf_op jit(solution)/shard_map/ending/pallas_call | solution.py:2462
